TPU v7x, 256 devices: a whole 4x4x8 slice. The times are simulated.
256 devices in a mesh: mem: 32 (over z_lo, y, core), lon: 8 (over z_hi, x).
Axes of the slice: x: 4, y: 4, z: 8 (z_hi: 2, z_lo: 4; z = z_hi * 4 + z_lo), core: 2. Of those that a mesh axis runs over, the one named last changes fastest.
Arguments:
- ensemble: bfloat16 [64, 2, 256, 1024], P('mem', None, None, 'lon'), may hold values from -6 to 6
- controls_start: float32 [64, 2, 256, 1024], P('mem', None, None, 'lon'), may hold values from -6 to 6
- kappa_east: float32 [2, 256, 1024], P(None, None, 'lon'), may hold values from 0.02 to 0.24
- kappa_north: float32 [2, 256, 1024], P(None, None, 'lon'), may hold values from 0.02 to 0.24
- innovation: float32 [2, 256, 1024], P(None, 'mem', 'lon'), may hold values from -6 to 6
- obs_mask: int32 [2, 256, 1024], P(None, 'mem', 'lon'), may hold values 0 or 1
- gauge_index: int32 [2, 256, 1024], P(None, 'mem', 'lon'), may hold values from 0 to 63
- gauge_precision: float32 [64], replicated, may hold values from 0.25 to 4
Outputs:
- controls: float32 [64, 2, 256, 1024], P('mem', None, None, 'lon')
- increment: float32 [2, 256, 1024], P(None, 'mem', 'lon')
All inputs are finite; a program needn't handle non-finite values. No bound on the sum of `obs_mask` on one device may be relied on, other than what follows from the above.
Results may differ from a plain program's by a relative error of at most 0.0003.
Values sent between devices are 32-bit elements; how exact they have to be, the bound alone decides.
No kernel may reach another device: no remote copies, remote signals or barrier semaphores. Data moves between devices by JAX's collectives and lax.ppermute only.
A program may use at most 64 MiB of HBM per device.

v0:
```python
import jax
import jax.numpy as jnp
from jax import lax
from jax.sharding import PartitionSpec as P

STEPS = 6
ITERS = 2
GAUGES = 64


step_size = 0.5


def padded(cells, sides, width):
    for axis, dim in sides:
        count = lax.axis_size(axis)
        head = lax.slice_in_dim(cells, 0, width, axis=dim)
        tail = lax.slice_in_dim(cells, cells.shape[dim] - width, cells.shape[dim], axis=dim)
        cells = jnp.concatenate(
            [
                lax.ppermute(tail, axis, [(i, (i + 1) % count) for i in range(count)]),
                cells,
                lax.ppermute(head, axis, [((i + 1) % count, i) for i in range(count)]),
            ],
            axis=dim,
        )
    return cells


def split_up(value, dim, peers):
    before, after = (value.shape[:dim], value.shape[dim + 1 :])
    return jnp.moveaxis(value.reshape(*before, peers, -1, *after), dim, 0)


def summed_on_arrival(value, axis, dim):
    parts = split_up(value, dim, lax.axis_size(axis))
    arrived = lax.all_to_all(parts, axis, split_axis=0, concat_axis=0, tiled=True)
    return arrived.sum(axis=0)


def copy_for_each(value, axis):
    copies = jnp.broadcast_to(value, (lax.axis_size(axis), *value.shape))
    return lax.all_to_all(copies, axis, split_axis=0, concat_axis=0, tiled=True)


def in_order(parts, dim):
    shape = list(parts.shape[1:])
    shape[dim] *= parts.shape[0]
    return jnp.moveaxis(parts, 0, dim).reshape(shape)


def gathered_copies(value, axis, dim):
    parts = copy_for_each(value, axis)
    return in_order(parts, dim)


def advance(extended, region):
    east_coef = region[0]
    north_coef = region[1][..., 1:-1]
    east_flux = east_coef[..., :-1] * (extended[..., 1:] - extended[..., :-1])
    inner = extended[..., 1:-1]
    north_flux = north_coef[..., :-1, :] * (inner[..., 1:, :] - inner[..., :-1, :])
    zero_row = jnp.zeros_like(inner[..., :1, :])
    upper = jnp.concatenate([north_flux, zero_row], axis=-2)
    lower = jnp.concatenate([zero_row, north_flux], axis=-2)
    return inner + east_flux[..., 1:] - east_flux[..., :-1] + upper - lower


def diffuse(values, coefs):
    extended = padded(values, (("lon", 3),), STEPS)
    for section in range(STEPS):
        extent = extended.shape[3]
        extended = advance(extended, coefs[..., section : section + extent])
    return extended


def body(
    ensemble,
    controls_start,
    kappa_east,
    kappa_north,
    innovation,
    obs_mask,
    gauge_index,
    gauge_precision,
):
    inv_root = float(lax.axis_size("mem") * ensemble.shape[0]) ** (-0.5)
    coefs = padded(jnp.stack([kappa_east, kappa_north]), (("lon", 3),), STEPS)
    labels = jnp.arange(GAUGES, dtype=jnp.int32)
    matches = gauge_index[None] == labels[:, None, None, None]
    precision = jnp.sum(jnp.where(matches, gauge_precision[:, None, None, None], 0.0), axis=0)
    weight = precision * obs_mask.astype(jnp.float32)
    controls = controls_start
    increment = jnp.zeros_like(innovation)
    for iteration in range(ITERS):
        smooth = diffuse(controls, coefs)
        partial_sum = inv_root * jnp.sum(ensemble * smooth, axis=0)
        increment = summed_on_arrival(partial_sum, "mem", 1)
        forcing = gathered_copies(weight * (increment - innovation), "mem", 1)
        gradient = diffuse(inv_root * ensemble * forcing, coefs)
        controls = controls - step_size * (controls + gradient)
    return (controls, increment)


def solution(mesh):
    in_specs = (
        P("mem", None, None, "lon"),
        P("mem", None, None, "lon"),
        P(None, None, "lon"),
        P(None, None, "lon"),
        P(None, "mem", "lon"),
        P(None, "mem", "lon"),
        P(None, "mem", "lon"),
        P(),
    )
    out_specs = (P("mem", None, None, "lon"), P(None, "mem", "lon"))
    return jax.shard_map(body, mesh=mesh, in_specs=in_specs, out_specs=out_specs, check_vma=False)
```

profile of v0, /device:TPU:7, one launch (start us, length us, event | category | flops | bytes accessed | tf_op | source)
XLA Modules:
  0.0 265.6 jit_solution(856431605634616527)
XLA Ops:
  0.6 1.5 slice_maximum_fusion
  2.2 6.9 %collective-permute-start.2 = (f32[2,2,256,6]{3,2,1,0:T(8,128)S(1)}, f32[2,2,256,6]{3,2,1,0:T(8,128)S(1)}, u32[]{:S(2)}, u32[]{:S(2)}) collective-permute-start(f32[2,2,256,6]{3,2,1,0:T(8,128)S(1)} %get-tuple-element.20), channel_id=1, source_target_pairs={{0,1},{1,2},{2,3},{3,4},{4,5},{5,6},{6,7},{7,0},{8,9},{9,10},{10,1... | collective-permute-start | bytes 73736 | tf_op jit(solution)/shard_map/ppermute | solution.py:21
  9.3 7.6 %collective-permute-start = (f32[2,2,256,6]{3,2,1,0:T(8,128)S(1)}, f32[2,2,256,6]{3,2,1,0:T(8,128)S(1)}, u32[]{:S(2)}, u32[]{:S(2)}) collective-permute-start(f32[2,2,256,6]{3,2,1,0:T(8,128)S(1)} %get-tuple-element.22), channel_id=1, source_target_pairs={{0,1},{1,2},{2,3},{3,4},{4,5},{5,6},{6,7},{7,0},{8,9},{9,10},{10,1... | collective-permute-start | bytes 73736 | tf_op jit(solution)/shard_map/ppermute | solution.py:21
  17.0 4.9 %collective-permute-done.2 = f32[2,2,256,6]{3,2,1,0:T(8,128)S(1)} collective-permute-done((f32[2,2,256,6]{3,2,1,0:T(8,128)S(1)}, f32[2,2,256,6]{3,2,1,0:T(8,128)S(1)}, u32[]{:S(2)}, u32[]{:S(2)}) %collective-permute-start.2) | collective-permute-done | bytes 24608 | tf_op jit(solution)/shard_map/ppermute | solution.py:21
  21.9 8.0 %collective-permute-done.3 = f32[2,2,256,6]{3,2,1,0:T(8,128)S(1)} collective-permute-done((f32[2,2,256,6]{3,2,1,0:T(8,128)S(1)}, f32[2,2,256,6]{3,2,1,0:T(8,128)S(1)}, u32[]{:S(2)}, u32[]{:S(2)}) %collective-permute-start.3) | collective-permute-done | bytes 24608 | tf_op jit(solution)/shard_map/ppermute | solution.py:23
  33.3 3.8 %collective-permute-done = f32[2,2,256,6]{3,2,1,0:T(8,128)S(1)} collective-permute-done((f32[2,2,256,6]{3,2,1,0:T(8,128)S(1)}, f32[2,2,256,6]{3,2,1,0:T(8,128)S(1)}, u32[]{:S(2)}, u32[]{:S(2)}) %collective-permute-start) | collective-permute-done | bytes 24608 | tf_op jit(solution)/shard_map/ppermute | solution.py:21
  37.1 8.1 %collective-permute-done.1 = f32[2,2,256,6]{3,2,1,0:T(8,128)S(1)} collective-permute-done((f32[2,2,256,6]{3,2,1,0:T(8,128)S(1)}, f32[2,2,256,6]{3,2,1,0:T(8,128)S(1)}, u32[]{:S(2)}, u32[]{:S(2)}) %collective-permute-start.1) | collective-permute-done | bytes 24608 | tf_op jit(solution)/shard_map/ppermute | solution.py:23
  46.1 0.6 fusion.80
  46.7 0.6 fusion.82
  47.7 0.6 fusion.76
  48.3 0.6 fusion.78
  49.3 0.6 fusion.72
  49.9 0.6 fusion.74
  50.8 0.6 fusion.68
  51.4 0.6 fusion.70
  52.4 0.6 fusion.64
  53.0 0.6 fusion.66
  55.3 0.7 copy.14
  56.1 23.5 %all-to-all-start = ((f32[32,2,8,128]{3,2,1,0:T(8,128)}), f32[32,2,8,128]{3,2,1,0:T(8,128)}, u32[]{:S(2)}, u32[]{:S(2)}) async-start(f32[32,2,8,128]{3,2,1,0:T(8,128)} %copy.14), calls=%async_computation | async-start | bytes 524288 | tf_op jit(solution)/shard_map/all_to_all | solution.py:37
  79.8 10.9 %all-to-all-done = f32[32,2,8,128]{3,2,1,0:T(8,128)} async-done(((f32[32,2,8,128]{3,2,1,0:T(8,128)}), f32[32,2,8,128]{3,2,1,0:T(8,128)}, u32[]{:S(2)}, u32[]{:S(2)}) %all-to-all-start) | async-done | bytes 262176 | tf_op jit(solution)/shard_map/all_to_all | solution.py:37
  90.7 1.0 reduce_sum.47
  91.7 14.7 %all_to_all.20 = f32[32,2,8,128]{3,2,1,0:T(8,128)S(1)} all-to-all(f32[32,2,8,128]{3,2,1,0:T(8,128)S(1)} %broadcast_in_dim.18), channel_id=1, replica_groups=mesh['mem'=32,'lon'=8] {'mem'}, dimensions={0} | all-to-all | bytes 524288 | tf_op jit(solution)/shard_map/all_to_all | solution.py:43
  106.5 0.9 copy-done.20
  107.8 1.4 collective-permute-start.5
  109.2 17.3 %collective-permute-done.4 = f32[2,2,256,6]{3,2,1,0:T(8,128)S(1)} collective-permute-done((f32[2,2,256,6]{3,2,1,0:T(8,128)S(1)}, f32[2,2,256,6]{3,2,1,0:T(8,128)S(1)}, u32[]{:S(2)}, u32[]{:S(2)}) %collective-permute-start.4) | collective-permute-done | bytes 24608 | tf_op jit(solution)/shard_map/ppermute | solution.py:21
  126.5 7.9 %collective-permute-done.5 = f32[2,2,256,6]{3,2,1,0:T(8,128)S(1)} collective-permute-done((f32[2,2,256,6]{3,2,1,0:T(8,128)S(1)}, f32[2,2,256,6]{3,2,1,0:T(8,128)S(1)}, u32[]{:S(2)}, u32[]{:S(2)}) %collective-permute-start.5) | collective-permute-done | bytes 24608 | tf_op jit(solution)/shard_map/ppermute | solution.py:23
  135.3 0.6 fusion.59
  135.9 0.6 fusion.61
  137.3 0.6 fusion.55
  137.9 0.6 fusion.57
  139.3 0.6 fusion.51
  141.3 0.6 fusion.47
  141.9 0.6 fusion.49
  143.3 0.6 fusion.43
  143.9 0.6 fusion.45
  145.2 0.7 copy-done.18
  147.1 1.1 collective-permute-start.7
  148.2 10.9 %collective-permute-done.6 = f32[2,2,256,6]{3,2,1,0:T(8,128)S(1)} collective-permute-done((f32[2,2,256,6]{3,2,1,0:T(8,128)S(1)}, f32[2,2,256,6]{3,2,1,0:T(8,128)S(1)}, u32[]{:S(2)}, u32[]{:S(2)}) %collective-permute-start.6) | collective-permute-done | bytes 24608 | tf_op jit(solution)/shard_map/ppermute | solution.py:21
  159.2 6.5 %collective-permute-done.7 = f32[2,2,256,6]{3,2,1,0:T(8,128)S(1)} collective-permute-done((f32[2,2,256,6]{3,2,1,0:T(8,128)S(1)}, f32[2,2,256,6]{3,2,1,0:T(8,128)S(1)}, u32[]{:S(2)}, u32[]{:S(2)}) %collective-permute-start.7) | collective-permute-done | bytes 24608 | tf_op jit(solution)/shard_map/ppermute | solution.py:23
  166.5 0.6 fusion.38
  167.1 0.6 fusion.40
  168.0 0.6 fusion.34
  168.7 0.6 fusion.36
  169.6 0.6 fusion.30
  171.2 0.6 fusion.26
  171.8 0.6 fusion.28
  172.7 0.6 fusion.22
  173.4 0.6 fusion.24
  175.1 29.0 %all_to_all.21 = f32[32,2,8,128]{3,2,1,0:T(8,128)} all-to-all(f32[32,2,8,128]{3,2,1,0:T(8,128)S(1)} %copy.16), channel_id=1, replica_groups=mesh['mem'=32,'lon'=8] {'mem'}, dimensions={0} | all-to-all | bytes 524288 | tf_op jit(solution)/shard_map/all_to_all | solution.py:37
  204.1 1.0 reduce_sum.49
  205.7 14.7 %all_to_all.22 = f32[32,2,8,128]{3,2,1,0:T(8,128)S(1)} all-to-all(f32[32,2,8,128]{3,2,1,0:T(8,128)S(1)} %broadcast_in_dim.19), channel_id=1, replica_groups=mesh['mem'=32,'lon'=8] {'mem'}, dimensions={0} | all-to-all | bytes 524288 | tf_op jit(solution)/shard_map/all_to_all | solution.py:43
  220.5 0.9 copy-done.21
  222.0 1.4 collective-permute-start.9
  223.4 21.0 %collective-permute-done.8 = f32[2,2,256,6]{3,2,1,0:T(8,128)S(1)} collective-permute-done((f32[2,2,256,6]{3,2,1,0:T(8,128)S(1)}, f32[2,2,256,6]{3,2,1,0:T(8,128)S(1)}, u32[]{:S(2)}, u32[]{:S(2)}) %collective-permute-start.8) | collective-permute-done | bytes 24608 | tf_op jit(solution)/shard_map/ppermute | solution.py:21
  244.4 8.3 %collective-permute-done.9 = f32[2,2,256,6]{3,2,1,0:T(8,128)S(1)} collective-permute-done((f32[2,2,256,6]{3,2,1,0:T(8,128)S(1)}, f32[2,2,256,6]{3,2,1,0:T(8,128)S(1)}, u32[]{:S(2)}, u32[]{:S(2)}) %collective-permute-start.9) | collective-permute-done | bytes 24608 | tf_op jit(solution)/shard_map/ppermute | solution.py:23
  253.5 0.6 fusion.17
  254.2 0.6 fusion.19
  255.6 0.6 fusion.13
  258.2 0.6 fusion.11
  259.6 0.6 fusion.5
  260.2 0.7 fusion.7
  262.2 0.6 fusion.3
  263.6 0.7 copy-done.16
  264.3 1.1 fusion.91
  (128 shorter events, 26.0 us)
Async XLA Ops:
  0.6 8.4 %copy-start.17 = (f32[2,2,256,128]{3,2,1,0:T(8,128)S(1)}, f32[2,2,256,128]{3,2,1,0:T(8,128)}, u32[]{:S(2)}) copy-start(f32[2,2,256,128]{3,2,1,0:T(8,128)} %param.9) | copy-start | bytes 1572868
  2.2 19.7 %collective-permute-start.2 = (f32[2,2,256,6]{3,2,1,0:T(8,128)S(1)}, f32[2,2,256,6]{3,2,1,0:T(8,128)S(1)}, u32[]{:S(2)}, u32[]{:S(2)}) collective-permute-start(f32[2,2,256,6]{3,2,1,0:T(8,128)S(1)} %get-tuple-element.20), channel_id=1, source_target_pairs={{0,1},{1,2},{2,3},{3,4},{4,5},{5,6},{6,7},{7,0},{8,9},{9,10},{10,1... | collective-permute-start | bytes 73736 | tf_op jit(solution)/shard_map/ppermute | solution.py:21
  9.1 20.8 %copy-start.22 = (f32[2,256,128]{2,1,0:T(8,128)S(1)}, f32[2,256,128]{2,1,0:T(8,128)}, u32[]{:S(2)}) copy-start(f32[2,256,128]{2,1,0:T(8,128)} %param.11) | copy-start | bytes 786436
  9.1 20.8 %copy-start.23 = (f32[2,256,128]{2,1,0:T(8,128)S(1)}, f32[2,256,128]{2,1,0:T(8,128)}, u32[]{:S(2)}) copy-start(f32[2,256,128]{2,1,0:T(8,128)} %param.10) | copy-start | bytes 786436
  9.1 20.8 %collective-permute-start.3 = (f32[2,2,256,6]{3,2,1,0:T(8,128)S(1)}, f32[2,2,256,6]{3,2,1,0:T(8,128)S(1)}, u32[]{:S(2)}, u32[]{:S(2)}) collective-permute-start(f32[2,2,256,6]{3,2,1,0:T(8,128)S(1)} %get-tuple-element.21), channel_id=1, source_target_pairs={{1,0},{2,1},{3,2},{4,3},{5,4},{6,5},{7,6},{0,7},{9,8},{10,9},{11,1... | collective-permute-start | bytes 73736 | tf_op jit(solution)/shard_map/ppermute | solution.py:23
  9.3 27.8 %collective-permute-start = (f32[2,2,256,6]{3,2,1,0:T(8,128)S(1)}, f32[2,2,256,6]{3,2,1,0:T(8,128)S(1)}, u32[]{:S(2)}, u32[]{:S(2)}) collective-permute-start(f32[2,2,256,6]{3,2,1,0:T(8,128)S(1)} %get-tuple-element.22), channel_id=1, source_target_pairs={{0,1},{1,2},{2,3},{3,4},{4,5},{5,6},{6,7},{7,0},{8,9},{9,10},{10,1... | collective-permute-start | bytes 73736 | tf_op jit(solution)/shard_map/ppermute | solution.py:21
  16.8 28.4 %collective-permute-start.1 = (f32[2,2,256,6]{3,2,1,0:T(8,128)S(1)}, f32[2,2,256,6]{3,2,1,0:T(8,128)S(1)}, u32[]{:S(2)}, u32[]{:S(2)}) collective-permute-start(f32[2,2,256,6]{3,2,1,0:T(8,128)S(1)} %get-tuple-element.23), channel_id=1, source_target_pairs={{1,0},{2,1},{3,2},{4,3},{5,4},{6,5},{7,6},{0,7},{9,8},{10,9},{11,1... | collective-permute-start | bytes 73736 | tf_op jit(solution)/shard_map/ppermute | solution.py:23
  30.7 18.2 %copy-start.3 = (f32[2,256,136]{2,1,0:T(8,128)}, f32[2,256,136]{2,1,0:T(8,128)S(1)}, u32[]{:S(2)}) copy-start(f32[2,256,136]{2,1,0:T(8,128)S(1)} %get-tuple-element.9) | copy-start | bytes 835588
  31.4 15.9 %copy-start.9 = (f32[2,256,138]{2,1,0:T(8,128)}, f32[2,256,138]{2,1,0:T(8,128)S(1)}, u32[]{:S(2)}) copy-start(f32[2,256,138]{2,1,0:T(8,128)S(1)} %get-tuple-element.11) | copy-start | bytes 847876
  31.7 18.7 %copy-start.6 = (f32[2,256,134]{2,1,0:T(8,128)}, f32[2,256,134]{2,1,0:T(8,128)S(1)}, u32[]{:S(2)}) copy-start(f32[2,256,134]{2,1,0:T(8,128)S(1)} %get-tuple-element.7) | copy-start | bytes 823300
  31.8 13.9 %copy-start.12 = (f32[2,256,140]{2,1,0:T(8,128)}, f32[2,256,140]{2,1,0:T(8,128)S(1)}, u32[]{:S(2)}) copy-start(f32[2,256,140]{2,1,0:T(8,128)S(1)} %get-tuple-element.13) | copy-start | bytes 860164
  32.2 19.9 %copy-start = (f32[2,256,132]{2,1,0:T(8,128)}, f32[2,256,132]{2,1,0:T(8,128)S(1)}, u32[]{:S(2)}) copy-start(f32[2,256,132]{2,1,0:T(8,128)S(1)} %get-tuple-element.5) | copy-start | bytes 811012
  54.0 1.0 copy-start.19
  56.1 23.5 %copy-start.27 = (s32[2,8,128]{2,1,0:T(8,128)S(1)}, s32[2,8,128]{2,1,0:T(8,128)}, u32[]{:S(2)}) copy-start(s32[2,8,128]{2,1,0:T(8,128)} %param.14) | copy-start | bytes 24580
  56.1 23.5 %copy-start.28 = (f32[64]{0:T(128)S(1)}, f32[64]{0:T(128)}, u32[]{:S(2)}) copy-start(f32[64]{0:T(128)} %param.15) | copy-start | bytes 772
  56.1 34.6 %all-to-all-start = ((f32[32,2,8,128]{3,2,1,0:T(8,128)}), f32[32,2,8,128]{3,2,1,0:T(8,128)}, u32[]{:S(2)}, u32[]{:S(2)}) async-start(f32[32,2,8,128]{3,2,1,0:T(8,128)} %copy.14), calls=%async_computation | async-start | bytes 524288 | tf_op jit(solution)/shard_map/all_to_all | solution.py:37
  79.7 12.0 %copy-start.24 = (f32[2,8,128]{2,1,0:T(8,128)S(1)}, f32[2,8,128]{2,1,0:T(8,128)}, u32[]{:S(2)}) copy-start(f32[2,8,128]{2,1,0:T(8,128)} %param.12) | copy-start | bytes 24580
  79.8 11.9 %copy-start.25 = (s32[2,8,128]{2,1,0:T(8,128)S(1)}, s32[2,8,128]{2,1,0:T(8,128)}, u32[]{:S(2)}) copy-start(s32[2,8,128]{2,1,0:T(8,128)} %param.13) | copy-start | bytes 24580
  106.4 1.0 copy-start.20
  107.7 18.9 %collective-permute-start.4 = (f32[2,2,256,6]{3,2,1,0:T(8,128)S(1)}, f32[2,2,256,6]{3,2,1,0:T(8,128)S(1)}, u32[]{:S(2)}, u32[]{:S(2)}) collective-permute-start(f32[2,2,256,6]{3,2,1,0:T(8,128)S(1)} %get-tuple-element.18), channel_id=1, source_target_pairs={{0,1},{1,2},{2,3},{3,4},{4,5},{5,6},{6,7},{7,0},{8,9},{9,10},{10,1... | collective-permute-start | bytes 73736 | tf_op jit(solution)/shard_map/ppermute | solution.py:21
  107.8 27.2 %copy-start.13 = (f32[2,256,140]{2,1,0:T(8,128)S(1)}, f32[2,256,140]{2,1,0:T(8,128)}, u32[]{:S(2)}) copy-start(f32[2,256,140]{2,1,0:T(8,128)} %copy-done.12) | copy-start | bytes 860164
  107.8 26.7 %collective-permute-start.5 = (f32[2,2,256,6]{3,2,1,0:T(8,128)S(1)}, f32[2,2,256,6]{3,2,1,0:T(8,128)S(1)}, u32[]{:S(2)}, u32[]{:S(2)}) collective-permute-start(f32[2,2,256,6]{3,2,1,0:T(8,128)S(1)} %get-tuple-element.19), channel_id=1, source_target_pairs={{1,0},{2,1},{3,2},{4,3},{5,4},{6,5},{7,6},{0,7},{9,8},{10,9},{11,1... | collective-permute-start | bytes 73736 | tf_op jit(solution)/shard_map/ppermute | solution.py:23
  135.9 1.0 copy-start.10
  137.9 1.0 copy-start.4
  139.9 1.0 copy-start.7
  141.9 1.0 copy-start.1
  144.9 1.0 copy-start.18
  146.3 19.3 %copy-start.15 = (f32[2,2,256,128]{3,2,1,0:T(8,128)}, f32[2,2,256,128]{3,2,1,0:T(8,128)S(1)}, u32[]{:S(2)}) copy-start(f32[2,2,256,128]{3,2,1,0:T(8,128)S(1)} %fusion.100) | copy-start | bytes 1572868
  146.5 12.6 %collective-permute-start.6 = (f32[2,2,256,6]{3,2,1,0:T(8,128)S(1)}, f32[2,2,256,6]{3,2,1,0:T(8,128)S(1)}, u32[]{:S(2)}, u32[]{:S(2)}) collective-permute-start(f32[2,2,256,6]{3,2,1,0:T(8,128)S(1)} %get-tuple-element.16), channel_id=1, source_target_pairs={{0,1},{1,2},{2,3},{3,4},{4,5},{5,6},{6,7},{7,0},{8,9},{9,10},{10,1... | collective-permute-start | bytes 73736 | tf_op jit(solution)/shard_map/ppermute | solution.py:21
  147.1 18.5 %collective-permute-start.7 = (f32[2,2,256,6]{3,2,1,0:T(8,128)S(1)}, f32[2,2,256,6]{3,2,1,0:T(8,128)S(1)}, u32[]{:S(2)}, u32[]{:S(2)}) collective-permute-start(f32[2,2,256,6]{3,2,1,0:T(8,128)S(1)} %get-tuple-element.17), channel_id=1, source_target_pairs={{1,0},{2,1},{3,2},{4,3},{5,4},{6,5},{7,6},{0,7},{9,8},{10,9},{11,1... | collective-permute-start | bytes 73736 | tf_op jit(solution)/shard_map/ppermute | solution.py:23
  205.1 0.6 copy-start.26
  220.4 1.0 copy-start.21
  221.7 22.8 %collective-permute-start.8 = (f32[2,2,256,6]{3,2,1,0:T(8,128)S(1)}, f32[2,2,256,6]{3,2,1,0:T(8,128)S(1)}, u32[]{:S(2)}, u32[]{:S(2)}) collective-permute-start(f32[2,2,256,6]{3,2,1,0:T(8,128)S(1)} %get-tuple-element.14), channel_id=1, source_target_pairs={{0,1},{1,2},{2,3},{3,4},{4,5},{5,6},{6,7},{7,0},{8,9},{9,10},{10,1... | collective-permute-start | bytes 73736 | tf_op jit(solution)/shard_map/ppermute | solution.py:21
  222.0 31.2 %copy-start.14 = (f32[2,256,140]{2,1,0:T(8,128)S(1)}, f32[2,256,140]{2,1,0:T(8,128)}, u32[]{:S(2)}) copy-start(f32[2,256,140]{2,1,0:T(8,128)} %copy-done.12) | copy-start | bytes 860164
  222.0 30.7 %collective-permute-start.9 = (f32[2,2,256,6]{3,2,1,0:T(8,128)S(1)}, f32[2,2,256,6]{3,2,1,0:T(8,128)S(1)}, u32[]{:S(2)}, u32[]{:S(2)}) collective-permute-start(f32[2,2,256,6]{3,2,1,0:T(8,128)S(1)} %get-tuple-element.15), channel_id=1, source_target_pairs={{1,0},{2,1},{3,2},{4,3},{5,4},{6,5},{7,6},{0,7},{9,8},{10,9},{11,1... | collective-permute-start | bytes 73736 | tf_op jit(solution)/shard_map/ppermute | solution.py:23
  254.2 1.0 copy-start.11
  256.2 1.0 copy-start.5
  258.2 1.0 copy-start.8
  260.2 1.0 copy-start.2
  263.2 1.0 copy-start.16
where the time goes:
time: 270 us; the launch traced here: 266 us
  waiting for transfers between devices  108 us (40%)
  blocking collectives  58.4 us (22%)
  starting transfers between devices  43.1 us (16%)
  other arithmetic  42.6 us (16%)
  local copies, waits for them, and re-layouts  12.3 us (5%)
    ppermute x5, waiting for transfers between devices, padded(): lax.ppermute(tail, axis, [(i, (i + 1) % count) for i in range(count)])  57.9 us
    ppermute x5, waiting for transfers between devices, padded(): lax.ppermute(head, axis, [((i + 1) % count, i) for i in range(count)])  38.9 us
    all_to_all x2, blocking collectives, copy_for_each(): return lax.all_to_all(copies, axis, split_axis=0, concat_axis=0, tiled=True)  29.4 us
    all_to_all x1, blocking collectives, summed_on_arrival(): lax.all_to_all(parts, axis, split_axis=0, concat_axis=0, tiled=True)  29 us
    all_to_all x1, starting transfers between devices, summed_on_arrival(): lax.all_to_all(parts, axis, split_axis=0, concat_axis=0, tiled=True)  23.5 us
    ppermute x5, starting transfers between devices, padded(): lax.ppermute(tail, axis, [(i, (i + 1) % count) for i in range(count)])  15.4 us
    mul x24, other arithmetic, advance(): north_coef[..., :-1, :] * (inner[..., 1:, :] - inner[..., :-1, :])  13.6 us
    sub x20, other arithmetic, advance(): return inner + east_flux[..., 1:] - east_flux[..., :-1] + upper - lower  12.3 us
  transfers between devices with their start and end apart: 11, of which 11 were waited for; matrix products, arithmetic and copies ran while one was open for 1% of the time, Pallas kernels for 0%

commit v1 on v0

v1 whole, which is shorter than its diff:
```python
import jax
import jax.numpy as jnp
from jax import lax
from jax.experimental import pallas as pl
from jax.experimental.pallas import tpu as pltpu
from jax.sharding import PartitionSpec as P

STEPS = 6
GAUGES = 64
step_size = 0.5

BAND = 128
OFF = 32
COLS = BAND + 2 * OFF
REACH = 3 * STEPS
HALO = 4 * STEPS
UNIT = 8
SENT = 2 * HALO + REACH + 2


def tiles(start, count):
    if isinstance(start, int):
        return pl.ds(8 * start, 8 * count)
    return pl.ds(pl.multiple_of(8 * start, 8), 8 * count)


def get(ref, start, count):
    return ref[tiles(start, count), :].reshape(count, 8, 128)


def put(ref, start, value):
    ref[tiles(start, value.shape[0]), :] = value.reshape(-1, 128)


def sublane():
    return lax.broadcasted_iota(jnp.int32, (1, 8, 128), 1)


def lane():
    return lax.broadcasted_iota(jnp.int32, (1, 8, 128), 2)


def for_blocks(lo, hi, work):
    count = -(-(hi - lo) // UNIT)

    def step(block, carry):
        work(lo + UNIT * block)
        return carry

    lax.fori_loop(0, count, step, 0)


def diffuse(source, spare, same, other, east, lo, hi):
    upper = sublane() >= 4
    for section in range(STEPS):
        lo, hi = lo + 1, hi - 1
        src, dst = (source, spare) if section % 2 == 0 else (spare, source)

        def work(at, src=src, dst=dst):
            values = get(src, at - 1, UNIT + 2)
            flux = get(east, at - 1, UNIT + 1) * (values[1:] - values[:-1])
            inner = values[1:-1]
            pair = pltpu.roll(inner, 4, 1)
            next_pair = jnp.where(upper, pltpu.roll(pair, 127, 2), pltpu.roll(pair, 1, 2))
            change = get(same, at, UNIT) * (pair - inner) + get(other, at, UNIT) * (next_pair - inner)
            put(dst, at, inner + (flux[1:] - flux[:-1]) + change)

        for_blocks(lo, hi, work)


def prepare_kernel(controls, ensemble, kappa_east, kappa_north, innovation, mask, gauge, precision,
                   c_out, k_out, e_out, w_out, right, left, wide):
    for member in range(2):
        for level in range(2):
            for parity in range(2):
                row = 4 * parity + 2 * member + level
                part = controls[member, level, pl.ds(parity, 128, stride=2), :]
                c_out[pl.ds(row, 128, stride=8), :] = part.T
                if parity == 0:
                    wide[...] = ensemble[member, level].astype(jnp.float32)
                e_out[pl.ds(row, 128, stride=8), :] = wide[pl.ds(parity, 128, stride=2), :].T
    for kind, kappa in enumerate((kappa_east, kappa_north)):
        for level in range(2):
            for parity in range(2):
                row = 4 * parity + 2 * kind + level
                k_out[pl.ds(row, 128, stride=8), :] = kappa[level, pl.ds(parity, 128, stride=2), :].T
    at = 0
    for part, width in ((c_out, HALO), (k_out, HALO), (e_out, REACH)):
        put(right, at, get(part, BAND - width, width))
        put(left, at, get(part, 0, width))
        at += width
    index = gauge[...]
    found = jnp.zeros(index.shape, jnp.float32)
    for label in range(GAUGES):
        found = jnp.where(index == label, precision[0, label], found)
    weight = found * mask[...].astype(jnp.float32)
    w_out[...] = weight
    lanes = lax.broadcasted_iota(jnp.int32, (8, 128), 1)
    for value in (weight, innovation[...]):
        to_right = jnp.zeros((8, 128), jnp.float32)
        to_left = jnp.zeros((8, 128), jnp.float32)
        for level in range(2):
            spot = 64 * level
            moved = pltpu.roll(value[level], (spot + REACH) % 128, 1)
            to_right = jnp.where((lanes >= spot) & (lanes < spot + REACH), moved, to_right)
            spot = 64 * level + 32
            moved = pltpu.roll(value[level], spot, 1)
            to_left = jnp.where((lanes >= spot) & (lanes < spot + REACH), moved, to_left)
        put(right, at, to_right[None])
        put(left, at, to_left[None])
        at += 1


def extend(band, from_left, from_right, out, at, width):
    put(out, OFF - width, get(from_left, at, width))
    put(out, OFF + BAND, get(from_right, at, width))
    out[tiles(OFF, BAND), :] = band[...]


def sum_members(values, ensemble, product, plain, out, blocks):
    def work(at):
        term = get(ensemble, at, UNIT) * get(values, at, UNIT)
        put(product, at, term + pltpu.roll(term, 6, 1))

    for_blocks(OFF - 24, OFF + BAND + 24, work)
    for parity in range(2):
        edges = []
        for level in range(2):
            row = 4 * parity + level
            part = product[pl.ds(8 * OFF + row, 128, stride=8), :]
            plain[level, pl.ds(parity, 128, stride=2), :] = part.T
            edges.append(product[pl.ds(8 * (OFF - REACH) + row, 32, stride=8), :])
            edges.append(product[pl.ds(8 * (OFF + BAND) + row, 32, stride=8), :])
        plain[2, pl.ds(parity, 128, stride=2), :] = jnp.concatenate(edges, axis=0).T
    for tile in range(3):
        out[:, tile] = plain[tile].reshape(blocks, 8, 128)


def spread(parts, plain, forcing):
    for tile in range(3):
        plain[tile] = parts[:, tile].reshape(256, 128)
    for parity in range(2):
        edges = plain[2, pl.ds(parity, 128, stride=2), :].T
        for level in range(2):
            band = plain[level, pl.ds(parity, 128, stride=2), :].T
            for member in range(2):
                row = 4 * parity + 2 * member + level
                left = edges[64 * level : 64 * level + 24]
                right = edges[64 * level + 32 : 64 * level + 56]
                forcing[pl.ds(8 * (OFF - REACH) + row, 24, stride=8), :] = left
                forcing[pl.ds(8 * (OFF + BAND) + row, 24, stride=8), :] = right
                forcing[pl.ds(8 * OFF + row, 128, stride=8), :] = band


def first_kernel(c_in, k_in, e_in, w_in, innovation, from_left, from_right,
                 out, c_out, e_out, same, other, east, w_out, i_out, values, spare, plain):
    blocks = out.shape[0]
    extend(c_in, from_left, from_right, c_out, 0, HALO)
    extend(k_in, from_left, from_right, spare, HALO, HALO)
    extend(e_in, from_left, from_right, e_out, 2 * HALO, REACH)
    upper = sublane() >= 4
    second = sublane() % 4 >= 2
    edge = (upper & (lane() == 127)) | (~upper & (lane() == 0))

    def coefs(at):
        both = get(spare, at, UNIT)
        put(east, at, jnp.where(second, pltpu.roll(both, 2, 1), both))
        north = jnp.where(second, both, pltpu.roll(both, 6, 1))
        swapped = pltpu.roll(north, 4, 1)
        put(same, at, jnp.where(upper, swapped, north))
        put(other, at, jnp.where(edge, 0.0, jnp.where(upper, north, pltpu.roll(swapped, 1, 2))))
        put(values, at, get(c_out, at, UNIT))

    for_blocks(OFF - HALO, OFF + BAND + HALO, coefs)
    for row, (band, result) in enumerate(((w_in, w_out), (innovation, i_out))):
        at = 2 * HALO + REACH + row
        result[:2] = band[...]
        result[2:] = get(from_left, at, 1) + get(from_right, at, 1)
    diffuse(values, spare, same, other, east, OFF - HALO, OFF + BAND + HALO)
    sum_members(values, e_out, spare, plain, out, blocks)


def forcing_kernel(parts, weight, innovation, out, increment, *, scale):
    total = parts[0]
    for block in range(1, parts.shape[0]):
        total = total + parts[block]
    total = scale * total
    increment[...] = total[:2]
    forcing = weight[...] * (total - innovation[...])
    for block in range(out.shape[0]):
        out[block] = forcing


def middle_kernel(parts, c_in, e_in, same, other, east, out, c_out, values, spare, plain, *, scale):
    blocks = out.shape[0]
    spread(parts, plain, values)

    def start(at):
        put(values, at, scale * get(e_in, at, UNIT) * get(values, at, UNIT))

    for_blocks(OFF - REACH, OFF + BAND + REACH, start)
    diffuse(values, spare, same, other, east, OFF - REACH, OFF + BAND + REACH)

    def update(at):
        new = get(c_in, at, UNIT)
        new = new - step_size * (new + get(values, at, UNIT))
        put(c_out, at, new)
        put(values, at, new)

    for_blocks(OFF - 2 * STEPS, OFF + BAND + 2 * STEPS, update)
    diffuse(values, spare, same, other, east, OFF - 2 * STEPS, OFF + BAND + 2 * STEPS)
    sum_members(values, e_in, spare, plain, out, blocks)


def last_kernel(parts, c_in, e_in, same, other, east, out, values, spare, plain, *, scale):
    spread(parts, plain, values)

    def start(at):
        put(values, at, scale * get(e_in, at, UNIT) * get(values, at, UNIT))

    for_blocks(OFF - STEPS, OFF + BAND + STEPS, start)
    diffuse(values, spare, same, other, east, OFF - STEPS, OFF + BAND + STEPS)

    def update(at):
        new = get(c_in, at, UNIT)
        put(values, at, new - step_size * (new + get(values, at, UNIT)))

    for_blocks(OFF, OFF + BAND, update)
    for member in range(2):
        for level in range(2):
            for parity in range(2):
                row = 4 * parity + 2 * member + level
                part = values[pl.ds(8 * OFF + row, 128, stride=8), :]
                out[member, level, pl.ds(parity, 128, stride=2), :] = part.T


def call(kernel, outs, scratch, name, *args):
    return pl.pallas_call(
        kernel,
        out_shape=[jax.ShapeDtypeStruct(shape, jnp.float32) for shape in outs],
        in_specs=[pl.BlockSpec(memory_space=pltpu.VMEM)] * len(args),
        out_specs=[pl.BlockSpec(memory_space=pltpu.VMEM)] * len(outs),
        scratch_shapes=[pltpu.VMEM(shape, jnp.float32) for shape in scratch],
        name=name,
    )(*args)


def swap(parts):
    return lax.all_to_all(parts, "mem", split_axis=0, concat_axis=0, tiled=True)


def body(ensemble, controls_start, kappa_east, kappa_north, innovation, obs_mask, gauge_index, gauge_precision):
    blocks = lax.axis_size("mem")
    bands = lax.axis_size("lon")
    scale = float(blocks * ensemble.shape[0]) ** (-0.5)
    band, wide, plain = (8 * BAND, 128), (8 * COLS, 128), (3, 256, 128)
    parcel, parts = (8 * SENT, 128), (blocks, 3, 8, 128)
    c, k, e, w, right, left = call(
        prepare_kernel, (band, band, band, innovation.shape, parcel, parcel), ((256, 128),), "prepare",
        controls_start, ensemble, kappa_east, kappa_north, innovation, obs_mask, gauge_index,
        gauge_precision.reshape(1, GAUGES),
    )
    from_left = lax.ppermute(right, "lon", [(i, (i + 1) % bands) for i in range(bands)])
    from_right = lax.ppermute(left, "lon", [((i + 1) % bands, i) for i in range(bands)])
    sums, c, e, same, other, east, weight, innov = call(
        first_kernel, (parts, wide, wide, wide, wide, wide, (3, 8, 128), (3, 8, 128)), (wide, wide, plain), "first",
        c, k, e, w, innovation, from_left, from_right,
    )

    def forced(sums):
        kernel = lambda *refs: forcing_kernel(*refs, scale=scale)
        return call(kernel, (parts, innovation.shape), (), "forcing", swap(sums), weight, innov)

    forcing, _ = forced(sums)
    kernel = lambda *refs: middle_kernel(*refs, scale=scale)
    sums, c = call(kernel, (parts, wide), (wide, wide, plain), "middle", swap(forcing), c, e, same, other, east)
    forcing, increment = forced(sums)
    kernel = lambda *refs: last_kernel(*refs, scale=scale)
    (controls,) = call(
        kernel, (controls_start.shape,), (wide, wide, plain), "last", swap(forcing), c, e, same, other, east
    )
    return controls, increment


def solution(mesh):
    in_specs = (
        P("mem", None, None, "lon"),
        P("mem", None, None, "lon"),
        P(None, None, "lon"),
        P(None, None, "lon"),
        P(None, "mem", "lon"),
        P(None, "mem", "lon"),
        P(None, "mem", "lon"),
        P(),
    )
    out_specs = (P("mem", None, None, "lon"), P(None, "mem", "lon"))
    return jax.shard_map(body, mesh=mesh, in_specs=in_specs, out_specs=out_specs, check_vma=False)
```

time: 270 us -> 166 us (0.61); the launches traced: 266 us -> 165 us
  waiting for transfers between devices: 108 us -> 14.5 us
  Pallas kernels: 0 us -> 62 us
  other arithmetic: 42.6 us -> 0 us
  starting transfers between devices: 43.1 us -> 6.83 us
  blocking collectives: 58.4 us -> 80.6 us
  local copies, waits for them, and re-layouts: 12.3 us -> 0.72 us
    ppermute x10 -> x2, waiting for transfers between devices: 96.7 us -> 14.5 us  [the longest x1 7.97 us: body(): lax.ppermute(left, 'lon', [((i + 1) % bands, i) for i in range(bands)])]
    pallas_call x0 -> x6, Pallas kernels: none -> 62 us  [call(): pl.pallas_call(kernel, out_shape=[jax.ShapeDtypeStruct(shape, jnp.float32...]
    all_to_all x1 -> x0, starting transfers between devices: 23.5 us -> none  [summed_on_arrival(): lax.all_to_all(parts, axis, split_axis=0, concat_axis=0, tiled=True)]
    all_to_all x3 -> x4, blocking collectives: 58.4 us -> 80.6 us  [swap(): return lax.all_to_all(parts, 'mem', split_axis=0, concat_axis=0, tiled=True)]
    mul x52 -> x0, other arithmetic: 22 us -> none  [the longest x24 13.6 us: advance(): north_coef[..., :-1, :] * (inner[..., 1:, :] - inner[..., :-1, :])]
    sub x22 -> x0, other arithmetic: 13.8 us -> none  [the longest x20 12.3 us: advance(): return inner + east_flux[..., 1:] - east_flux[..., :-1] + upper - lower]
    ppermute x10 -> x2, starting transfers between devices: 19.6 us -> 6.83 us  [the longest x1 6.82 us: body(): lax.ppermute(right, 'lon', [(i, (i + 1) % bands) for i in range(bands)])]
    all_to_all x1 -> x0, waiting for transfers between devices: 10.9 us -> none  [summed_on_arrival(): lax.all_to_all(parts, axis, split_axis=0, concat_axis=0, tiled=True)]
  transfers between devices with their start and end apart: 11 -> 2, of which waited for: 11 -> 2; matrix products, arithmetic and copies ran while one was open for 1% -> 0% of each run, Pallas kernels for 0% -> 0%
where the time goes in v1:
time: 166 us; the launch traced here: 165 us
  blocking collectives  80.6 us (49%)
  Pallas kernels  62 us (37%)
  waiting for transfers between devices  14.5 us (9%)
  starting transfers between devices  6.83 us (4%)
    all_to_all x4, blocking collectives, swap(): return lax.all_to_all(parts, 'mem', split_axis=0, concat_axis=0, tiled=True)  80.6 us
    pallas_call x6, Pallas kernels, call(): pl.pallas_call(kernel, out_shape=[jax.ShapeDtypeStruct(shape, jnp.float32...  62 us
    ppermute x1, waiting for transfers between devices, body(): lax.ppermute(left, 'lon', [((i + 1) % bands, i) for i in range(bands)])  7.97 us
    ppermute x1, starting transfers between devices, body(): lax.ppermute(right, 'lon', [(i, (i + 1) % bands) for i in range(bands)])  6.82 us
    ppermute x1, waiting for transfers between devices, body(): lax.ppermute(right, 'lon', [(i, (i + 1) % bands) for i in range(bands)])  6.54 us
  transfers between devices with their start and end apart: 2, of which 2 were waited for; matrix products, arithmetic and copies ran while one was open for 0% of the time, Pallas kernels for 0%

profile of v1, /device:TPU:7, one launch (start us, length us, event | category | flops | bytes accessed | tf_op | source)
XLA Modules:
  0.0 165.3 jit_solution(17599224099825520462)
XLA Ops:
  0.6 3.2 %prepare.1 = (f32[1024,128]{1,0:T(8,128)}, f32[1024,128]{1,0:T(8,128)}, f32[1024,128]{1,0:T(8,128)}, f32[2,8,128]{2,1,0:T(8,128)}, f32[544,128]{1,0:T(8,128)}, /*index=5*/f32[544,128]{1,0:T(8,128)}) custom-call(f32[2,2,256,128]{3,2,1,0:T(8,128)} %controls.1, bf16[2,2,256,128]{3,2,1,0:T(8,128)(2,1)} %ensemble.1, f32[2,256,128]{2,1,0:T(8,128)} %kappa_east.1, ...), custom_call_target="tpu_custom_call" | custom-call | tf_op jit(solution)/shard_map/prepare/pallas_call | solution.py:238
  3.8 6.8 %collective-permute-start = (f32[544,128]{1,0:T(8,128)}, f32[544,128]{1,0:T(8,128)S(1)}, u32[]{:S(2)}, u32[]{:S(2)}) collective-permute-start(f32[544,128]{1,0:T(8,128)} %get-tuple-element.25), channel_id=1, source_target_pairs={{0,1},{1,2},{2,3},{3,4},{4,5},{5,6},{6,7},{7,0},{8,9},{9,10},{10,1... | collective-permute-start | bytes 835592 | tf_op jit(solution)/shard_map/ppermute | solution.py:263
  10.6 0.0 collective-permute-start.1
  10.6 6.5 %collective-permute-done.from_left = f32[544,128]{1,0:T(8,128)S(1)} collective-permute-done((f32[544,128]{1,0:T(8,128)}, f32[544,128]{1,0:T(8,128)S(1)}, u32[]{:S(2)}, u32[]{:S(2)}) %collective-permute-start) | collective-permute-done | bytes 278560 | tf_op jit(solution)/shard_map/ppermute | solution.py:263
  17.2 0.0 copy-start
  17.2 8.0 %collective-permute-done.1.from_right = f32[544,128]{1,0:T(8,128)S(1)} collective-permute-done((f32[544,128]{1,0:T(8,128)}, f32[544,128]{1,0:T(8,128)S(1)}, u32[]{:S(2)}, u32[]{:S(2)}) %collective-permute-start.1) | collective-permute-done | bytes 278560 | tf_op jit(solution)/shard_map/ppermute | solution.py:264
  25.2 0.0 copy-start.1
  25.2 0.0 copy-done
  25.2 0.7 copy-done.1
  25.9 17.3 %first.1 = (f32[32,3,8,128]{3,2,1,0:T(8,128)}, f32[1536,128]{1,0:T(8,128)}, f32[1536,128]{1,0:T(8,128)}, f32[1536,128]{1,0:T(8,128)}, f32[1536,128]{1,0:T(8,128)...) custom-call(f32[1024,128]{1,0:T(8,128)} %get-tuple-element.21.c_in, ...), custom_call_target="tpu_custom_call" | custom-call | tf_op jit(solution)/shard_map/first/pallas_call | solution.py:238
  43.2 26.2 %all_to_all.20.refs_0_ = f32[32,3,8,128]{3,2,1,0:T(8,128)} all-to-all(f32[32,3,8,128]{3,2,1,0:T(8,128)} %get-tuple-element.27), channel_id=1, replica_groups=mesh['mem'=32,'lon'=8] {'mem'}, dimensions={0} | all-to-all | bytes 786432 | tf_op jit(solution)/shard_map/all_to_all | solution.py:249
  69.3 1.8 %forcing.2 = (f32[32,3,8,128]{3,2,1,0:T(8,128)}, f32[2,8,128]{2,1,0:T(8,128)}) custom-call(f32[32,3,8,128]{3,2,1,0:T(8,128)} %all_to_all.20.refs_0_, f32[3,8,128]{2,1,0:T(8,128)} %get-tuple-element.28.refs_1_, f32[3,8,128]{2,1,0:T(8,128)} %get-tuple-element.29.refs_2_), custom_call_target="tpu_custom_call" | custom-call | tf_op jit(solution)/shard_map/forcing/pallas_call | solution.py:238
  71.2 18.1 %all_to_all.21.refs_0_ = f32[32,3,8,128]{3,2,1,0:T(8,128)} all-to-all(f32[32,3,8,128]{3,2,1,0:T(8,128)} %get-tuple-element.30), channel_id=1, replica_groups=mesh['mem'=32,'lon'=8] {'mem'}, dimensions={0} | all-to-all | bytes 786432 | tf_op jit(solution)/shard_map/all_to_all | solution.py:249
  89.3 25.0 %middle.1 = (f32[32,3,8,128]{3,2,1,0:T(8,128)}, f32[1536,128]{1,0:T(8,128)}) custom-call(f32[32,3,8,128]{3,2,1,0:T(8,128)} %all_to_all.21.refs_0_, f32[1536,128]{1,0:T(8,128)} %get-tuple-element.31.refs_1_, f32[1536,128]{1,0:T(8,128)} %get-tuple-element.32.refs_2_, f32[1536,128]{1,0:T(8,128)} %get-tuple-element.33.refs_3_, ...), custom_call_target="tpu_custom_call" | custom-call | tf_op jit(solution)/shard_map/middle/pallas_call | solution.py:238
  114.2 18.1 %all_to_all.22.refs_0_ = f32[32,3,8,128]{3,2,1,0:T(8,128)} all-to-all(f32[32,3,8,128]{3,2,1,0:T(8,128)} %get-tuple-element.36), channel_id=1, replica_groups=mesh['mem'=32,'lon'=8] {'mem'}, dimensions={0} | all-to-all | bytes 786432 | tf_op jit(solution)/shard_map/all_to_all | solution.py:249
  132.4 1.8 %forcing.3 = (f32[32,3,8,128]{3,2,1,0:T(8,128)}, f32[2,8,128]{2,1,0:T(8,128)}) custom-call(f32[32,3,8,128]{3,2,1,0:T(8,128)} %all_to_all.22.refs_0_, f32[3,8,128]{2,1,0:T(8,128)} %get-tuple-element.28.refs_1_, f32[3,8,128]{2,1,0:T(8,128)} %get-tuple-element.29.refs_2_), custom_call_target="tpu_custom_call" | custom-call | tf_op jit(solution)/shard_map/forcing/pallas_call | solution.py:238
  134.2 18.1 %all_to_all.23.refs_0_ = f32[32,3,8,128]{3,2,1,0:T(8,128)} all-to-all(f32[32,3,8,128]{3,2,1,0:T(8,128)} %get-tuple-element.37), channel_id=1, replica_groups=mesh['mem'=32,'lon'=8] {'mem'}, dimensions={0} | all-to-all | bytes 786432 | tf_op jit(solution)/shard_map/all_to_all | solution.py:249
  152.4 12.9 %last.1 = f32[2,2,256,128]{3,2,1,0:T(8,128)} custom-call(f32[32,3,8,128]{3,2,1,0:T(8,128)} %all_to_all.23.refs_0_, f32[1536,128]{1,0:T(8,128)} %get-tuple-element.38.refs_1_, f32[1536,128]{1,0:T(8,128)} %get-tuple-element.32.refs_2_, f32[1536,128]{1,0:T(8,128)} %get-tuple-element.33.refs_3_, f32[1536,128]{1,0:T(8,128)} %get-tuple-element.34.refs_4_, ...), custom_call_target="tpu_custom_call" | custom-call | tf_op jit(solution)/shard_map/last/pallas_call | solution.py:238
Async XLA Ops:
  3.8 13.4 %collective-permute-start = (f32[544,128]{1,0:T(8,128)}, f32[544,128]{1,0:T(8,128)S(1)}, u32[]{:S(2)}, u32[]{:S(2)}) collective-permute-start(f32[544,128]{1,0:T(8,128)} %get-tuple-element.25), channel_id=1, source_target_pairs={{0,1},{1,2},{2,3},{3,4},{4,5},{5,6},{6,7},{7,0},{8,9},{9,10},{10,1... | collective-permute-start | bytes 835592 | tf_op jit(solution)/shard_map/ppermute | solution.py:263
  10.6 14.5 %collective-permute-start.1 = (f32[544,128]{1,0:T(8,128)}, f32[544,128]{1,0:T(8,128)S(1)}, u32[]{:S(2)}, u32[]{:S(2)}) collective-permute-start(f32[544,128]{1,0:T(8,128)} %get-tuple-element.26), channel_id=1, source_target_pairs={{1,0},{2,1},{3,2},{4,3},{5,4},{6,5},{7,6},{0,7},{9,8},{10,9},{11,1... | collective-permute-start | bytes 835592 | tf_op jit(solution)/shard_map/ppermute | solution.py:264
  17.2 8.0 %copy-start = (f32[544,128]{1,0:T(8,128)}, f32[544,128]{1,0:T(8,128)S(1)}, u32[]{:S(2)}) copy-start(f32[544,128]{1,0:T(8,128)S(1)} %collective-permute-done.from_left) | copy-start | bytes 835588
  25.2 0.7 copy-start.1

commit v2 on v1

v2 whole, which is shorter than its diff:
```python
import jax
import jax.numpy as jnp
from jax import lax
from jax.experimental import pallas as pl
from jax.experimental.pallas import tpu as pltpu
from jax.sharding import PartitionSpec as P

STEPS = 6
GAUGES = 64
step_size = 0.5

UNROLL = True
BAND = 128
PAD = 8
HALO = 4 * STEPS
REACH = 3 * STEPS
SPAN = HALO + BAND // 2
SIZE = PAD + SPAN + PAD
UNIT = 8
SENT = 2 * HALO + REACH + 2


def tiles(place, count):
    if isinstance(place, int):
        return pl.ds(8 * (PAD + place), 8 * count)
    return pl.ds(pl.multiple_of(8 * (PAD + place), 8), 8 * count)


def get(ref, place, count):
    return ref[tiles(place, count), :].reshape(count, 8, 128)


def put(ref, place, value):
    ref[tiles(place, value.shape[0]), :] = value.reshape(-1, 128)


def rows(place, row, count):
    return pl.ds(8 * (PAD + place) + row, count, stride=8)


def lane_index():
    return lax.broadcasted_iota(jnp.int32, (1, 8, 128), 2)


def row_index():
    return lax.broadcasted_iota(jnp.int32, (1, 8, 128), 1)


def flipped(value):
    groups = value.reshape(-1, 8, 128)
    index = 7 - lax.broadcasted_iota(jnp.int32, groups.shape, 1)
    groups = jnp.take_along_axis(groups, index, axis=1)
    count = groups.shape[0]
    return jnp.concatenate([groups[count - 1 - i] for i in range(count)], axis=0)


def halves_of(band):
    return band[:64], flipped(band[64:])


def band_of(ref, row):
    first = ref[rows(HALO, row, 64), :]
    return jnp.concatenate([first, flipped(ref[rows(HALO, row + 4, 64), :])], axis=0)


def for_blocks(lo, work):
    count = -(-(SPAN - lo) // UNIT)
    first = SPAN - UNIT * count

    def step(block, carry):
        work(first + UNIT * block)
        return carry

    lax.fori_loop(0, count, step, 0)


def join(ref):
    put(ref, SPAN, pltpu.roll(get(ref, SPAN - 1, 1), 4, 1))


def diffuse(source, spare, east, same, other, lo):
    for parity in range(2):
        join(source.at[parity])
    for section in range(STEPS):
        lo += 1
        src, dst = (source, spare) if section % 2 == 0 else (spare, source)
        count = -(-(SPAN - lo) // UNIT)
        first = SPAN - UNIT * count

        def block(at, carry, src=src, dst=dst):
            ahead, *before = carry
            even, odd = (get(src.at[parity], at, UNIT + 1) for parity in range(2))
            across = get(other, at, UNIT) * (ahead - odd[:-1])
            back = pltpu.roll(across, 1, 2)
            next_ahead = pltpu.roll(get(src.at[0], at + UNIT, UNIT), 127, 2)
            within = get(same, at, UNIT) * (odd[:-1] - even[:-1])
            after = []
            for parity, values, north in ((1, odd, across - within), (0, even, None)):
                flux = get(east.at[parity], at, UNIT) * (values[1:] - values[:-1])
                change = flux - jnp.concatenate([before[parity], flux[:-1]], axis=0)
                if north is None:
                    north = within - back
                put(dst.at[parity], at, (values[:-1] + change) + north)
                after.insert(0, flux[-1:])
            return (next_ahead, *after)

        ahead = pltpu.roll(get(src.at[0], first, UNIT), 127, 2)
        before = [
            get(east.at[parity], first - 1, 1)
            * (get(src.at[parity], first, 1) - get(src.at[parity], first - 1, 1))
            for parity in range(2)
        ]
        carry = (ahead, *before)
        if UNROLL:
            for i in range(count):
                carry = block(first + UNIT * i, carry)
        else:
            carry = lax.fori_loop(0, count, lambda i, c, block=block, first=first: block(first + UNIT * i, c), carry)
        for parity in range(2):
            join(dst.at[parity])


def prepare_kernel(controls, ensemble, kappa_east, kappa_north, innovation, mask, gauge, precision,
                   c_out, k_out, e_out, w_out, first, second, wide):
    odd = lax.axis_index("lon") % 2 == 1

    def lay(values, parity, row, out):
        for half, part in enumerate(halves_of(values.T)):
            out[parity, rows(HALO, row + 4 * half, 64), :] = part

    for member in range(2):
        for level in range(2):
            row = 2 * member + level
            wide[...] = ensemble[member, level].astype(jnp.float32)
            for parity in range(2):
                lay(controls[member, level, pl.ds(parity, 128, stride=2), :], parity, row, c_out)
                lay(wide[pl.ds(parity, 128, stride=2), :], parity, row, e_out)
    for kind, kappa in enumerate((kappa_east, kappa_north)):
        for level in range(2):
            for parity in range(2):
                lay(kappa[level, pl.ds(parity, 128, stride=2), :], parity, 2 * kind + level, k_out)
    low = row_index() < 4
    at = 0

    def send(right, left):
        right, left = right.reshape(8, 128), left.reshape(8, 128)
        first[8 * at : 8 * (at + 1), :] = jnp.where(odd, right, left)
        second[8 * at : 8 * (at + 1), :] = jnp.where(odd, left, right)

    for part, width in ((c_out, HALO), (k_out, HALO), (e_out, REACH)):
        for place in range(HALO - width, HALO):
            one, two = (get(part.at[parity], 2 * HALO - 1 - place, 1) for parity in range(2))
            send(jnp.where(low, pltpu.roll(one, 4, 1), two), jnp.where(low, one, pltpu.roll(two, 4, 1)))
            at += 1
    index = gauge[...]
    found = jnp.zeros(index.shape, jnp.float32)
    for label in range(GAUGES):
        found = jnp.where(index == label, precision[0, label], found)
    weight = found * mask[...].astype(jnp.float32)
    w_out[...] = weight
    lanes = lax.broadcasted_iota(jnp.int32, (8, 128), 1)
    for value in (weight, innovation[...]):
        to_right = jnp.zeros((8, 128), jnp.float32)
        to_left = jnp.zeros((8, 128), jnp.float32)
        for level in range(2):
            place = lanes - 64 * level
            moved = jnp.take_along_axis(value[level], jnp.clip(BAND - HALO + place, 0, 127), axis=1)
            to_right = jnp.where((place >= HALO - REACH) & (place < HALO), moved, to_right)
            place = place - 32
            moved = jnp.take_along_axis(value[level], jnp.clip(HALO - 1 - place, 0, 127), axis=1)
            to_left = jnp.where((place >= HALO - REACH) & (place < HALO), moved, to_left)
        send(to_right, to_left)
        at += 1


def received(first, second, at):
    odd = lax.axis_index("lon") % 2 == 1
    one, two = (part[8 * at : 8 * (at + 1), :].reshape(1, 8, 128) for part in (first, second))
    return jnp.where(odd, two, one), jnp.where(odd, one, two)


def extend(band, first, second, out, at, width):
    low = row_index() < 4
    for place in range(HALO - width, HALO):
        one, two = received(first, second, at)
        put(out.at[0], place, jnp.where(low, one, pltpu.roll(two, 4, 1)))
        put(out.at[1], place, jnp.where(low, pltpu.roll(one, 4, 1), two))
        at += 1
    for parity in range(2):
        out[parity, tiles(HALO, SPAN - HALO), :] = band[parity, tiles(HALO, SPAN - HALO), :]


def block_rows(chip, own):
    core = lax.axis_index("mem") % 2
    if not own:
        core = 1 - core
    return pl.ds(pl.multiple_of(16 * chip + 8 * core, 8), 8)


def sum_members(values, ensemble, product, plain, mine, other_core, lo):
    def work(at):
        for parity in range(2):
            term = get(ensemble.at[parity], at, UNIT) * get(values.at[parity], at, UNIT)
            put(product.at[parity], at, term + pltpu.roll(term, 6, 1))

    for_blocks(lo, work)
    for parity in range(2):
        edges = []
        for level in range(2):
            plain[level, pl.ds(parity, 128, stride=2), :] = band_of(product.at[parity], level).T
            for half in range(2):
                edges.append(product[parity, rows(0, level + 4 * half, 32), :])
        plain[2, pl.ds(parity, 128, stride=2), :] = jnp.concatenate(edges, axis=0).T
    for tile in range(3):
        for chip in range(mine.shape[0]):
            mine[chip, tile] = plain[tile, block_rows(chip, True), :]
            other_core[chip, tile] = plain[tile, block_rows(chip, False), :]


def spread(mine, other_core, plain, forcing):
    for tile in range(3):
        for chip in range(mine.shape[0]):
            plain[tile, block_rows(chip, True), :] = mine[chip, tile]
            plain[tile, block_rows(chip, False), :] = other_core[chip, tile]
    for parity in range(2):
        edges = plain[2, pl.ds(parity, 128, stride=2), :].T
        for level in range(2):
            halves = halves_of(plain[level, pl.ds(parity, 128, stride=2), :].T)
            for half in range(2):
                edge = edges[64 * level + 32 * half : 64 * level + 32 * half + HALO]
                for member in range(2):
                    row = 4 * half + 2 * member + level
                    forcing[parity, rows(0, row, HALO), :] = edge
                    forcing[parity, rows(HALO, row, 64), :] = halves[half]


def first_kernel(c_in, k_in, e_in, w_in, innovation, near, far,
                 mine, other_core, c_out, e_out, east, same, other, w_out, i_out, values, spare, plain):
    extend(c_in, near, far, c_out, 0, HALO)
    extend(k_in, near, far, spare, HALO, HALO)
    extend(e_in, near, far, e_out, 2 * HALO, REACH)
    low = row_index() < 4
    second = row_index() % 4 >= 2
    last = lane_index() == 127
    for parity in range(2):
        join(spare.at[parity])

    def coefs(at):
        for parity in range(2):
            both = get(spare.at[parity], at, UNIT + 1)
            face = jnp.where(low, both[:-1], both[1:])
            put(east.at[parity], at, jnp.where(second, pltpu.roll(face, 2, 1), face))
            north = jnp.where(second, both[:-1], pltpu.roll(both[:-1], 6, 1))
            if parity == 0:
                put(same, at, north)
            else:
                put(other, at, jnp.where(last, 0.0, north))
            put(values.at[parity], at, get(c_out.at[parity], at, UNIT))

    for_blocks(0, coefs)
    for row, (band, result) in enumerate(((w_in, w_out), (innovation, i_out))):
        at = 2 * HALO + REACH + row
        result[:2] = band[...]
        result[2] = near[8 * at : 8 * (at + 1), :] + far[8 * at : 8 * (at + 1), :]
    diffuse(values, spare, east, same, other, 0)
    sum_members(values, e_out, spare, plain, mine, other_core, STEPS)


def forcing_kernel(parts, weight, innovation, out, increment, *, scale):
    total = parts[0]
    for block in range(1, parts.shape[0]):
        total = total + parts[block]
    total = scale * total
    increment[...] = total[:2]
    forcing = weight[...] * (total - innovation[...])
    for block in range(out.shape[0]):
        out[block] = forcing


def gradient(e_in, east, same, other, values, spare, scale, lo):
    def start(at):
        for parity in range(2):
            term = get(e_in.at[parity], at, UNIT) * get(values.at[parity], at, UNIT)
            put(values.at[parity], at, scale * term)

    for_blocks(lo, start)
    diffuse(values, spare, east, same, other, lo)


def middle_kernel(mine, other_core, c_in, e_in, east, same, other, mine_out, other_out, c_out, values, spare, plain, *, scale):
    spread(mine, other_core, plain, values)
    gradient(e_in, east, same, other, values, spare, scale, STEPS)

    def update(at):
        for parity in range(2):
            new = get(c_in.at[parity], at, UNIT)
            new = new - step_size * (new + get(values.at[parity], at, UNIT))
            put(c_out.at[parity], at, new)
            put(values.at[parity], at, new)

    for_blocks(2 * STEPS, update)
    diffuse(values, spare, east, same, other, 2 * STEPS)
    sum_members(values, e_in, spare, plain, mine_out, other_out, 3 * STEPS)


def last_kernel(mine, other_core, c_in, e_in, east, same, other, out, values, spare, plain, *, scale):
    spread(mine, other_core, plain, values)
    gradient(e_in, east, same, other, values, spare, scale, 3 * STEPS)

    def update(at):
        for parity in range(2):
            new = get(c_in.at[parity], at, UNIT)
            put(values.at[parity], at, new - step_size * (new + get(values.at[parity], at, UNIT)))

    for_blocks(HALO, update)
    for member in range(2):
        for level in range(2):
            for parity in range(2):
                part = band_of(values.at[parity], 2 * member + level)
                out[member, level, pl.ds(parity, 128, stride=2), :] = part.T


def call(kernel, outs, scratch, name, *args):
    return pl.pallas_call(
        kernel,
        out_shape=[jax.ShapeDtypeStruct(shape, jnp.float32) for shape in outs],
        in_specs=[pl.BlockSpec(memory_space=pltpu.VMEM)] * len(args),
        out_specs=[pl.BlockSpec(memory_space=pltpu.VMEM)] * len(outs),
        scratch_shapes=[pltpu.VMEM(shape, jnp.float32) for shape in scratch],
        name=name,
    )(*args)


def swap_chips(parts):
    size = lax.axis_size("mem")
    groups = [list(range(core, size, 2)) for core in range(2)]
    return lax.all_to_all(parts, "mem", split_axis=0, concat_axis=0, tiled=True, axis_index_groups=groups)


def swap_cores(part):
    return lax.ppermute(part, "mem", [(i, i ^ 1) for i in range(lax.axis_size("mem"))])


def swap_bands(part, odd_up):
    bands = lax.axis_size("lon")
    return lax.ppermute(part, "lon", [(i, (i + 1 if (i % 2 == 1) == odd_up else i - 1) % bands) for i in range(bands)])


def body(ensemble, controls_start, kappa_east, kappa_north, innovation, obs_mask, gauge_index, gauge_precision):
    chips = lax.axis_size("mem") // 2
    scale = float(lax.axis_size("mem") * ensemble.shape[0]) ** (-0.5)
    field, one, plain = (2, 8 * SIZE, 128), (8 * SIZE, 128), (3, 256, 128)
    parcel, parts = (8 * SENT, 128), (chips, 3, 8, 128)
    c, k, e, w, first, second = call(
        prepare_kernel, (field, field, field, innovation.shape, parcel, parcel), ((256, 128),), "prepare",
        controls_start, ensemble, kappa_east, kappa_north, innovation, obs_mask, gauge_index,
        gauge_precision.reshape(1, GAUGES),
    )
    near, far = swap_bands(first, True), swap_bands(second, False)
    mine, theirs, c, e, east, same, other, weight, innov = call(
        first_kernel, (parts, parts, field, field, field, one, one, (3, 8, 128), (3, 8, 128)), (field, field, plain),
        "first", c, k, e, w, innovation, near, far,
    )

    def forced(mine, theirs):
        kernel = lambda *refs: forcing_kernel(*refs, scale=scale)
        sums = swap_chips(mine + swap_cores(theirs))
        forcing, increment = call(kernel, (parts, innovation.shape), (), "forcing", sums, weight, innov)
        mine = swap_chips(forcing)
        return mine, swap_cores(mine), increment

    mine, theirs, _ = forced(mine, theirs)
    kernel = lambda *refs: middle_kernel(*refs, scale=scale)
    mine, theirs, c = call(
        kernel, (parts, parts, field), (field, field, plain), "middle", mine, theirs, c, e, east, same, other
    )
    mine, theirs, increment = forced(mine, theirs)
    kernel = lambda *refs: last_kernel(*refs, scale=scale)
    (controls,) = call(
        kernel, (controls_start.shape,), (field, field, plain), "last", mine, theirs, c, e, east, same, other
    )
    return controls, increment


def solution(mesh):
    in_specs = (
        P("mem", None, None, "lon"),
        P("mem", None, None, "lon"),
        P(None, None, "lon"),
        P(None, None, "lon"),
        P(None, "mem", "lon"),
        P(None, "mem", "lon"),
        P(None, "mem", "lon"),
        P(),
    )
    out_specs = (P("mem", None, None, "lon"), P(None, "mem", "lon"))
    return jax.shard_map(body, mesh=mesh, in_specs=in_specs, out_specs=out_specs, check_vma=False)
```

time: 166 us -> 124 us (0.75)
  the two profiles are of different devices: /device:TPU:7 before, /device:TPU:1 now
where the time goes in v2:
time: 124 us
  blocking collectives  51.7 us (42%)
  Pallas kernels  34.5 us (28%)
  starting transfers between devices  16.7 us (13%)
  waiting for transfers between devices  16.1 us (13%)
  local copies, waits for them, and re-layouts  2.16 us (2%)
  other arithmetic  1.9 us (2%)
    all_to_all x4, blocking collectives, swap_chips(): lax.all_to_all(parts, 'mem', split_axis=0, concat_axis=0, tiled=True, axi...  51.7 us
    pallas_call x6, Pallas kernels, call(): pl.pallas_call(kernel, out_shape=[jax.ShapeDtypeStruct(shape, jnp.float32...  34.5 us
    ppermute x2, waiting for transfers between devices, swap_bands(): lax.ppermute(part, 'lon', [(i, (i + 1 if (i % 2 == 1) == odd_up else i -...  11.4 us
    ppermute x2, starting transfers between devices, swap_bands(): lax.ppermute(part, 'lon', [(i, (i + 1 if (i % 2 == 1) == odd_up else i -...  9.92 us
    ppermute x4, starting transfers between devices, swap_cores(): lax.ppermute(part, 'mem', [(i, i ^ 1) for i in range(lax.axis_size('mem'))])  6.78 us
    ppermute x4, waiting for transfers between devices, swap_cores(): lax.ppermute(part, 'mem', [(i, i ^ 1) for i in range(lax.axis_size('mem'))])  4.7 us
  transfers between devices with their start and end apart: 6, of which 5 were waited for; matrix products, arithmetic and copies ran while one was open for 0% of the time, Pallas kernels for 0%

profile of v2, /device:TPU:1, one launch (start us, length us, event | category | flops | bytes accessed | tf_op | source)
XLA Modules:
  0.0 123.7 jit_solution(14004983912780031274)
XLA Ops:
  0.6 3.4 %prepare.1 = (f32[2,832,128]{2,1,0:T(8,128)}, f32[2,832,128]{2,1,0:T(8,128)}, f32[2,832,128]{2,1,0:T(8,128)}, f32[2,8,128]{2,1,0:T(8,128)}, f32[544,128]{1,0:T(8,128)}, /*index=5*/f32[544,128]{1,0:T(8,128)}) custom-call(f32[2,2,256,128]{3,2,1,0:T(8,128)} %controls.1, bf16[2,2,256,128]{3,2,1,0:T(8,128)(2,1)} %ensemble.1, f32[2,256,128]{2,1,0:T(8,128)} %kappa_east.1, ...), custom_call_target="tpu_custom_call" | custom-call | tf_op jit(solution)/shard_map/prepare/pallas_call | solution.py:324
  4.0 9.9 %collective-permute-start = (f32[544,128]{1,0:T(8,128)}, f32[544,128]{1,0:T(8,128)S(1)}, u32[]{:S(2)}, u32[]{:S(2)}) collective-permute-start(f32[544,128]{1,0:T(8,128)} %get-tuple-element.27), channel_id=1, source_target_pairs={{0,7},{1,2},{2,1},{3,4},{4,3},{5,6},{6,5},{7,0},{8,15},{9,10},{10,... | collective-permute-start | bytes 835592 | tf_op jit(solution)/shard_map/ppermute | solution.py:346
  13.9 0.0 collective-permute-start.1
  13.9 11.4 %collective-permute-done.near = f32[544,128]{1,0:T(8,128)S(1)} collective-permute-done((f32[544,128]{1,0:T(8,128)}, f32[544,128]{1,0:T(8,128)S(1)}, u32[]{:S(2)}, u32[]{:S(2)}) %collective-permute-start) | collective-permute-done | bytes 278560 | tf_op jit(solution)/shard_map/ppermute | solution.py:346
  25.3 0.0 copy-start.2
  25.3 0.0 collective-permute-done.1.far
  25.3 0.0 copy-start.3
  25.3 0.7 copy-done.2
  26.0 0.1 copy-done.3
  26.1 8.9 %first.1 = (f32[16,3,8,128]{3,2,1,0:T(8,128)}, f32[16,3,8,128]{3,2,1,0:T(8,128)}, f32[2,832,128]{2,1,0:T(8,128)}, f32[2,832,128]{2,1,0:T(8,128)}, f32[2,832,128]...) custom-call(f32[2,832,128]{2,1,0:T(8,128)} %get-tuple-element.23.c_in, ...), custom_call_target="tpu_custom_call" | custom-call | tf_op jit(solution)/shard_map/first/pallas_call | solution.py:324
  35.0 1.7 %collective-permute-start.2 = (f32[16,3,8,128]{3,2,1,0:T(8,128)}, f32[16,3,8,128]{3,2,1,0:T(8,128)S(1)}, u32[]{:S(2)}, u32[]{:S(2)}) collective-permute-start(f32[16,3,8,128]{3,2,1,0:T(8,128)} %get-tuple-element.30), channel_id=1, source_target_pairs={{0,8},{8,0},{16,24},{24,16},{32,40},{40,32},{48,56},{56,48},{64,72... | collective-permute-start | bytes 589832 | tf_op jit(solution)/shard_map/ppermute | solution.py:341
  36.7 1.3 %collective-permute-done.2 = f32[16,3,8,128]{3,2,1,0:T(8,128)S(1)} collective-permute-done((f32[16,3,8,128]{3,2,1,0:T(8,128)}, f32[16,3,8,128]{3,2,1,0:T(8,128)S(1)}, u32[]{:S(2)}, u32[]{:S(2)}) %collective-permute-start.2) | collective-permute-done | bytes 196640 | tf_op jit(solution)/shard_map/ppermute | solution.py:341
  37.9 0.9 add.6
  38.9 15.1 %all_to_all.20.refs_0_ = f32[16,3,8,128]{3,2,1,0:T(8,128)} all-to-all(f32[16,3,8,128]{3,2,1,0:T(8,128)S(1)} %add.6), channel_id=1, replica_groups={{0,16,32,48,64,80,96,112,128,144,160,176,192,208,224,240},{8,24,40,56,7..., dimensions={0} | all-to-all | bytes 393216 | tf_op jit(solution)/shard_map/all_to_all | solution.py:337
  54.0 1.7 %forcing.2 = (f32[16,3,8,128]{3,2,1,0:T(8,128)}, f32[2,8,128]{2,1,0:T(8,128)}) custom-call(f32[16,3,8,128]{3,2,1,0:T(8,128)} %all_to_all.20.refs_0_, f32[3,8,128]{2,1,0:T(8,128)} %get-tuple-element.31.refs_1_, f32[3,8,128]{2,1,0:T(8,128)} %get-tuple-element.32.refs_2_), custom_call_target="tpu_custom_call" | custom-call | tf_op jit(solution)/shard_map/forcing/pallas_call | solution.py:324
  55.6 12.3 %all_to_all.21.refs_0_ = f32[16,3,8,128]{3,2,1,0:T(8,128)S(1)} all-to-all(f32[16,3,8,128]{3,2,1,0:T(8,128)} %get-tuple-element.33), channel_id=1, replica_groups={{0,16,32,48,64,80,96,112,128,144,160,176,192,208,224,240},{8,24,40,56,7..., dimensions={0} | all-to-all | bytes 393216 | tf_op jit(solution)/shard_map/all_to_all | solution.py:337
  67.9 0.0 copy-start.1
  67.9 2.4 %collective-permute-start.3 = (f32[16,3,8,128]{3,2,1,0:T(8,128)S(1)}, f32[16,3,8,128]{3,2,1,0:T(8,128)S(1)}, u32[]{:S(2)}, u32[]{:S(2)}) collective-permute-start(f32[16,3,8,128]{3,2,1,0:T(8,128)S(1)} %all_to_all.21.refs_0_), channel_id=1, source_target_pairs={{0,8},{8,0},{16,24},{24,16},{32,40},{40,32},{48,56},{56,48},{64,72... | collective-permute-start | bytes 589832 | tf_op jit(solution)/shard_map/ppermute | solution.py:341
  70.3 1.1 collective-permute-done.3.refs_1_
  71.3 0.0 copy-start.5
  71.3 0.0 copy-done.1
  71.3 0.7 copy-done.5
  72.0 12.3 %middle.1 = (f32[16,3,8,128]{3,2,1,0:T(8,128)}, f32[16,3,8,128]{3,2,1,0:T(8,128)}, f32[2,832,128]{2,1,0:T(8,128)}) custom-call(f32[16,3,8,128]{3,2,1,0:T(8,128)} %copy-done.1, f32[16,3,8,128]{3,2,1,0:T(8,128)} %copy-done.5, f32[2,832,128]{2,1,0:T(8,128)} %get-tuple-element.34.refs_2_, f32[2,832,128]{2,1,0:T(8,128)} %get-tuple-element.35.refs_3_, ...), custom_call_target="tpu_custom_call" | custom-call | tf_op jit(solution)/shard_map/middle/pallas_call | solution.py:324
  84.3 0.4 collective-permute-start.4
  84.6 1.3 %collective-permute-done.4 = f32[16,3,8,128]{3,2,1,0:T(8,128)S(1)} collective-permute-done((f32[16,3,8,128]{3,2,1,0:T(8,128)}, f32[16,3,8,128]{3,2,1,0:T(8,128)S(1)}, u32[]{:S(2)}, u32[]{:S(2)}) %collective-permute-start.4) | collective-permute-done | bytes 196640 | tf_op jit(solution)/shard_map/ppermute | solution.py:341
  85.9 0.9 add.7
  86.9 12.3 %all_to_all.22.refs_0_ = f32[16,3,8,128]{3,2,1,0:T(8,128)} all-to-all(f32[16,3,8,128]{3,2,1,0:T(8,128)S(1)} %add.7), channel_id=1, replica_groups={{0,16,32,48,64,80,96,112,128,144,160,176,192,208,224,240},{8,24,40,56,7..., dimensions={0} | all-to-all | bytes 393216 | tf_op jit(solution)/shard_map/all_to_all | solution.py:337
  99.2 1.7 %forcing.3 = (f32[16,3,8,128]{3,2,1,0:T(8,128)}, f32[2,8,128]{2,1,0:T(8,128)}) custom-call(f32[16,3,8,128]{3,2,1,0:T(8,128)} %all_to_all.22.refs_0_, f32[3,8,128]{2,1,0:T(8,128)} %get-tuple-element.31.refs_1_, f32[3,8,128]{2,1,0:T(8,128)} %get-tuple-element.32.refs_2_), custom_call_target="tpu_custom_call" | custom-call | tf_op jit(solution)/shard_map/forcing/pallas_call | solution.py:324
  100.8 12.1 %all_to_all.23.refs_0_ = f32[16,3,8,128]{3,2,1,0:T(8,128)S(1)} all-to-all(f32[16,3,8,128]{3,2,1,0:T(8,128)} %get-tuple-element.41), channel_id=1, replica_groups={{0,16,32,48,64,80,96,112,128,144,160,176,192,208,224,240},{8,24,40,56,7..., dimensions={0} | all-to-all | bytes 393216 | tf_op jit(solution)/shard_map/all_to_all | solution.py:337
  112.9 0.0 copy-start
  112.9 2.4 %collective-permute-start.5 = (f32[16,3,8,128]{3,2,1,0:T(8,128)S(1)}, f32[16,3,8,128]{3,2,1,0:T(8,128)S(1)}, u32[]{:S(2)}, u32[]{:S(2)}) collective-permute-start(f32[16,3,8,128]{3,2,1,0:T(8,128)S(1)} %all_to_all.23.refs_0_), channel_id=1, source_target_pairs={{0,8},{8,0},{16,24},{24,16},{32,40},{40,32},{48,56},{56,48},{64,72... | collective-permute-start | bytes 589832 | tf_op jit(solution)/shard_map/ppermute | solution.py:341
  115.3 1.1 collective-permute-done.5.refs_1_
  116.4 0.0 copy-start.4
  116.4 0.0 copy-done
  116.4 0.7 copy-done.4
  117.1 6.7 %last.1 = f32[2,2,256,128]{3,2,1,0:T(8,128)} custom-call(f32[16,3,8,128]{3,2,1,0:T(8,128)} %copy-done, f32[16,3,8,128]{3,2,1,0:T(8,128)} %copy-done.4, f32[2,832,128]{2,1,0:T(8,128)} %get-tuple-element.42.refs_2_, f32[2,832,128]{2,1,0:T(8,128)} %get-tuple-element.35.refs_3_, f32[2,832,128]{2,1,0:T(8,128)} %get-tuple-element.36.refs_4_, ...), custom_call_target="tpu_custom_call" | custom-call | tf_op jit(solution)/shard_map/last/pallas_call | solution.py:324
Async XLA Ops:
  4.0 21.3 %collective-permute-start = (f32[544,128]{1,0:T(8,128)}, f32[544,128]{1,0:T(8,128)S(1)}, u32[]{:S(2)}, u32[]{:S(2)}) collective-permute-start(f32[544,128]{1,0:T(8,128)} %get-tuple-element.27), channel_id=1, source_target_pairs={{0,7},{1,2},{2,1},{3,4},{4,3},{5,6},{6,5},{7,0},{8,15},{9,10},{10,... | collective-permute-start | bytes 835592 | tf_op jit(solution)/shard_map/ppermute | solution.py:346
  13.9 11.4 %collective-permute-start.1 = (f32[544,128]{1,0:T(8,128)}, f32[544,128]{1,0:T(8,128)S(1)}, u32[]{:S(2)}, u32[]{:S(2)}) collective-permute-start(f32[544,128]{1,0:T(8,128)} %get-tuple-element.28), channel_id=1, source_target_pairs={{0,1},{1,0},{2,3},{3,2},{4,5},{5,4},{6,7},{7,6},{8,9},{9,8},{10,11... | collective-permute-start | bytes 835592 | tf_op jit(solution)/shard_map/ppermute | solution.py:346
  25.3 0.7 copy-start.2
  25.3 0.8 copy-start.3
  35.0 3.0 %collective-permute-start.2 = (f32[16,3,8,128]{3,2,1,0:T(8,128)}, f32[16,3,8,128]{3,2,1,0:T(8,128)S(1)}, u32[]{:S(2)}, u32[]{:S(2)}) collective-permute-start(f32[16,3,8,128]{3,2,1,0:T(8,128)} %get-tuple-element.30), channel_id=1, source_target_pairs={{0,8},{8,0},{16,24},{24,16},{32,40},{40,32},{48,56},{56,48},{64,72... | collective-permute-start | bytes 589832 | tf_op jit(solution)/shard_map/ppermute | solution.py:341
  67.9 3.4 %copy-start.1 = (f32[16,3,8,128]{3,2,1,0:T(8,128)}, f32[16,3,8,128]{3,2,1,0:T(8,128)S(1)}, u32[]{:S(2)}) copy-start(f32[16,3,8,128]{3,2,1,0:T(8,128)S(1)} %all_to_all.21.refs_0_) | copy-start | bytes 589828
  67.9 3.4 %collective-permute-start.3 = (f32[16,3,8,128]{3,2,1,0:T(8,128)S(1)}, f32[16,3,8,128]{3,2,1,0:T(8,128)S(1)}, u32[]{:S(2)}, u32[]{:S(2)}) collective-permute-start(f32[16,3,8,128]{3,2,1,0:T(8,128)S(1)} %all_to_all.21.refs_0_), channel_id=1, source_target_pairs={{0,8},{8,0},{16,24},{24,16},{32,40},{40,32},{48,56},{56,48},{64,72... | collective-permute-start | bytes 589832 | tf_op jit(solution)/shard_map/ppermute | solution.py:341
  71.3 0.7 copy-start.5
  84.3 1.7 %collective-permute-start.4 = (f32[16,3,8,128]{3,2,1,0:T(8,128)}, f32[16,3,8,128]{3,2,1,0:T(8,128)S(1)}, u32[]{:S(2)}, u32[]{:S(2)}) collective-permute-start(f32[16,3,8,128]{3,2,1,0:T(8,128)} %get-tuple-element.40), channel_id=1, source_target_pairs={{0,8},{8,0},{16,24},{24,16},{32,40},{40,32},{48,56},{56,48},{64,72... | collective-permute-start | bytes 589832 | tf_op jit(solution)/shard_map/ppermute | solution.py:341
  112.9 3.4 %copy-start = (f32[16,3,8,128]{3,2,1,0:T(8,128)}, f32[16,3,8,128]{3,2,1,0:T(8,128)S(1)}, u32[]{:S(2)}) copy-start(f32[16,3,8,128]{3,2,1,0:T(8,128)S(1)} %all_to_all.23.refs_0_) | copy-start | bytes 589828
  112.9 3.4 %collective-permute-start.5 = (f32[16,3,8,128]{3,2,1,0:T(8,128)S(1)}, f32[16,3,8,128]{3,2,1,0:T(8,128)S(1)}, u32[]{:S(2)}, u32[]{:S(2)}) collective-permute-start(f32[16,3,8,128]{3,2,1,0:T(8,128)S(1)} %all_to_all.23.refs_0_), channel_id=1, source_target_pairs={{0,8},{8,0},{16,24},{24,16},{32,40},{40,32},{48,56},{56,48},{64,72... | collective-permute-start | bytes 589832 | tf_op jit(solution)/shard_map/ppermute | solution.py:341
  116.4 0.7 copy-start.4

commit v3 on v2

v3 whole, which is shorter than its diff:
```python
import jax
import jax.numpy as jnp
from jax import lax
from jax.experimental import pallas as pl
from jax.experimental.pallas import tpu as pltpu
from jax.sharding import PartitionSpec as P

STEPS = 6
GAUGES = 64
step_size = 0.5

BAND = 128
PAD = 1
HALO = 4 * STEPS
REACH = 3 * STEPS
SPAN = HALO + BAND // 2
SIZE = PAD + SPAN + PAD
UNIT = 8
SENT = 2 * HALO + REACH + 2


def tiles(place, count):
    if isinstance(place, int):
        return pl.ds(8 * (PAD + place), 8 * count)
    return pl.ds(pl.multiple_of(8 * (PAD + place), 8), 8 * count)


def get(ref, place, count):
    return ref[tiles(place, count), :].reshape(count, 8, 128)


def put(ref, place, value):
    ref[tiles(place, value.shape[0]), :] = value.reshape(-1, 128)


def rows(place, row, count):
    return pl.ds(8 * (PAD + place) + row, count, stride=8)


def lane_index():
    return lax.broadcasted_iota(jnp.int32, (1, 8, 128), 2)


def row_index():
    return lax.broadcasted_iota(jnp.int32, (1, 8, 128), 1)


def flipped(value):
    groups = value.reshape(-1, 8, 128)
    index = 7 - lax.broadcasted_iota(jnp.int32, groups.shape, 1)
    groups = jnp.take_along_axis(groups, index, axis=1)
    count = groups.shape[0]
    return jnp.concatenate([groups[count - 1 - i] for i in range(count)], axis=0)


def halves_of(band):
    return band[:64], flipped(band[64:])


def band_of(ref, row):
    first = ref[rows(HALO, row, 64), :]
    return jnp.concatenate([first, flipped(ref[rows(HALO, row + 4, 64), :])], axis=0)


def blocks_from(lo, hi=SPAN):
    return range(hi - UNIT * -(-(hi - lo) // UNIT), hi, UNIT)


def join(ref):
    put(ref, SPAN, pltpu.roll(get(ref, SPAN - 1, 1), 4, 1))


def diffuse(source, spare, east, same, other, spans, joined=True, before_step=None):
    def opening(src, first):
        before = []
        for parity in range(2):
            pair = get(src.at[parity], first - 1, 2)
            before.append(get(east.at[parity], first - 1, 1) * (pair[1:] - pair[:1]))
        return pltpu.roll(get(src.at[0], first, UNIT), 127, 2), *before

    if joined:
        for parity in range(2):
            join(source.at[parity])
    carry = opening(source, spans[0][0])
    for section, (first, end) in enumerate(spans):
        src, dst = (source, spare) if section % 2 == 0 else (spare, source)
        if before_step is not None:
            before_step(section, src)
        ahead, *before = carry
        for at in range(first, end, UNIT):
            even, odd = (get(src.at[parity], at, UNIT + 1) for parity in range(2))
            across = get(other, at, UNIT) * (ahead - odd[:-1])
            back = pltpu.roll(across, 1, 2)
            if at + UNIT < end:
                ahead = pltpu.roll(get(src.at[0], at + UNIT, UNIT), 127, 2)
            elif section + 1 < STEPS:
                carry = opening(dst, spans[section + 1][0])
            within = get(same, at, UNIT) * (odd[:-1] - even[:-1])
            for parity, values in ((1, odd), (0, even)):
                flux = get(east.at[parity], at, UNIT) * (values[1:] - values[:-1])
                change = flux - jnp.concatenate([before[parity], flux[:-1]], axis=0)
                north = across - within if parity else within - back
                put(dst.at[parity], at, (values[:-1] + change) + north)
                before[parity] = flux[-1:]
        if joined:
            for parity in range(2):
                join(dst.at[parity])


def inward(lo):
    return [(blocks_from(lo + step)[0], SPAN) for step in range(1, STEPS + 1)]


def edges_kernel(controls, ensemble, kappa_east, kappa_north, innovation, mask, gauge, precision,
                 w_out, i_out, first, second, right, left, wide):
    odd = lax.axis_index("lon") % 2 == 1

    def send(values, at, row):
        turned = values.T
        right[pl.ds(8 * at + row, HALO, stride=8), :] = turned[BAND - HALO :]
        left[pl.ds(8 * at + row, HALO, stride=8), :] = flipped(turned[:HALO])

    for member in range(2):
        for level in range(2):
            row = 2 * member + level
            wide[...] = ensemble[member, level].astype(jnp.float32)
            for parity in range(2):
                send(controls[member, level, pl.ds(parity, 128, stride=2), :], 0, 4 * parity + row)
                send(wide[pl.ds(parity, 128, stride=2), :], HALO + REACH, 4 * parity + row)
    for kind, kappa in enumerate((kappa_east, kappa_north)):
        for level in range(2):
            for parity in range(2):
                send(kappa[level, pl.ds(parity, 128, stride=2), :], HALO, 4 * parity + 2 * kind + level)
    index = gauge[...]
    found = jnp.zeros(index.shape, jnp.float32)
    for label in range(GAUGES):
        found = jnp.where(index == label, precision[0, label], found)
    weight = found * mask[...].astype(jnp.float32)
    w_out[...] = weight
    i_out[...] = innovation[...]
    lanes = lax.broadcasted_iota(jnp.int32, (8, 128), 1)
    at = 2 * HALO + REACH
    for value in (weight, innovation[...]):
        to_right = jnp.zeros((8, 128), jnp.float32)
        to_left = jnp.zeros((8, 128), jnp.float32)
        for level in range(2):
            place = lanes - 64 * level
            moved = jnp.take_along_axis(value[level], jnp.clip(BAND - HALO + place, 0, 127), axis=1)
            to_right = jnp.where((place >= HALO - REACH) & (place < HALO), moved, to_right)
            place = place - 32
            moved = jnp.take_along_axis(value[level], jnp.clip(HALO - 1 - place, 0, 127), axis=1)
            to_left = jnp.where((place >= HALO - REACH) & (place < HALO), moved, to_left)
        right[8 * at : 8 * (at + 1), :] = to_right
        left[8 * at : 8 * (at + 1), :] = to_left
        at += 1
    first[...] = jnp.where(odd, right[...], left[...])
    second[...] = jnp.where(odd, left[...], right[...])


def coefficients(raw, east, same, other, blocks):
    low = row_index() < 4
    second = row_index() % 4 >= 2
    last = lane_index() == 127
    for at in blocks:
        for parity in range(2):
            both = get(raw.at[parity], at, UNIT + 1)
            face = jnp.where(low, both[:-1], both[1:])
            put(east.at[parity], at, jnp.where(second, pltpu.roll(face, 2, 1), face))
            north = jnp.where(second, both[:-1], pltpu.roll(both[:-1], 6, 1))
            if parity == 0:
                put(same, at, north)
            else:
                put(other, at, jnp.where(last, 0.0, north))


def multiply(values, ensemble, product, blocks):
    for at in blocks:
        for parity in range(2):
            term = get(ensemble.at[parity], at, UNIT) * get(values.at[parity], at, UNIT)
            put(product.at[parity], at, term + pltpu.roll(term, 6, 1))


def inner_kernel(controls, ensemble, kappa_east, kappa_north,
                 c_out, e_out, east, same, other, product, saved, values, spare, raw, wide):
    def lay(values, parity, row, *outs):
        for half, part in enumerate(halves_of(values.T)):
            for out in outs:
                out[parity, rows(HALO, row + 4 * half, 64), :] = part

    for member in range(2):
        for level in range(2):
            row = 2 * member + level
            wide[...] = ensemble[member, level].astype(jnp.float32)
            for parity in range(2):
                lay(controls[member, level, pl.ds(parity, 128, stride=2), :], parity, row, c_out, values)
                lay(wide[pl.ds(parity, 128, stride=2), :], parity, row, e_out)
    for kind, kappa in enumerate((kappa_east, kappa_north)):
        for level in range(2):
            for parity in range(2):
                lay(kappa[level, pl.ds(parity, 128, stride=2), :], parity, 2 * kind + level, raw)
    for parity in range(2):
        join(raw.at[parity])
        saved[parity, pl.ds(16 * STEPS, 8), :] = raw[parity, tiles(HALO, 1), :]
    coefficients(raw, east, same, other, blocks_from(HALO))

    def save(section, src):
        for parity in range(2):
            saved[parity, pl.ds(16 * section, 16), :] = src[parity, tiles(HALO + section, 2), :]

    diffuse(values, spare, east, same, other, inward(HALO), before_step=save)
    multiply(values, e_out, product, blocks_from(HALO))


def copy_of(source, target, sem):
    return pltpu.make_async_copy(source, target, sem)


def received(near, far, at):
    odd = lax.axis_index("lon") % 2 == 1
    one, two = (part[8 * at : 8 * (at + 1), :].reshape(1, 8, 128) for part in (near, far))
    return jnp.where(odd, two, one), jnp.where(odd, one, two)


def outer(near, far, at, width, *outs):
    low = row_index() < 4
    for place in range(HALO - width, HALO):
        one, two = received(near, far, at)
        even = jnp.where(low, one, pltpu.roll(two, 4, 1))
        odd = jnp.where(low, pltpu.roll(one, 4, 1), two)
        for out in outs:
            put(out.at[0], place, even)
            put(out.at[1], place, odd)
        at += 1


def block_rows(chip, own):
    core = lax.axis_index("mem") % 2
    if not own:
        core = 1 - core
    return pl.ds(pl.multiple_of(16 * chip + 8 * core, 8), 8)


def lay_out(product, plain, mine, other_core):
    for parity in range(2):
        edges = []
        for level in range(2):
            plain[level, pl.ds(parity, 128, stride=2), :] = band_of(product.at[parity], level).T
            for half in range(2):
                edges.append(product[parity, rows(0, level + 4 * half, 32), :])
        plain[2, pl.ds(parity, 128, stride=2), :] = jnp.concatenate(edges, axis=0).T
    for tile in range(3):
        for chip in range(mine.shape[0]):
            mine[chip, tile] = plain[tile, block_rows(chip, True), :]
            other_core[chip, tile] = plain[tile, block_rows(chip, False), :]


def spread(mine, other_core, plain, forcing):
    for tile in range(3):
        for chip in range(mine.shape[0]):
            plain[tile, block_rows(chip, True), :] = mine[chip, tile]
            plain[tile, block_rows(chip, False), :] = other_core[chip, tile]
    for parity in range(2):
        edges = plain[2, pl.ds(parity, 128, stride=2), :].T
        for level in range(2):
            halves = halves_of(plain[level, pl.ds(parity, 128, stride=2), :].T)
            for half in range(2):
                edge = edges[64 * level + 32 * half : 64 * level + 32 * half + HALO]
                for member in range(2):
                    row = 4 * half + 2 * member + level
                    forcing[parity, rows(0, row, HALO), :] = edge
                    forcing[parity, rows(HALO, row, 64), :] = halves[half]


def outer_kernel(near, far, w_in, i_in, saved, e_hbm, east_hbm, same_hbm, other_hbm, product_hbm,
                 mine, other_core, w_out, i_out, c_far, e_far, east_far, same_far, other_far,
                 values, spare, plain, product, raw, c, e, east, same, other, sem_in, sem_out):
    edge, rest = tiles(HALO, UNIT), tiles(HALO + STEPS, SPAN - HALO - STEPS)
    fetched = [
        copy_of(source.at[..., edge, :], target.at[..., edge, :], sem_in.at[place])
        for place, (source, target) in enumerate(((e_hbm, e), (east_hbm, east), (same_hbm, same), (other_hbm, other)))
    ]
    fetched.append(copy_of(product_hbm.at[:, rest, :], product.at[:, rest, :], sem_in.at[4]))
    for copy in fetched:
        copy.start()
    outer(near, far, HALO, HALO, raw)
    for parity in range(2):
        raw[parity, tiles(HALO, 1), :] = saved[parity, pl.ds(16 * STEPS, 8), :]
    outer(near, far, 0, HALO, c, values)
    outer(near, far, 2 * HALO, REACH, e)
    for row, (band, result) in enumerate(((w_in, w_out), (i_in, i_out))):
        at = 2 * HALO + REACH + row
        result[:2] = band[...]
        result[2] = near[8 * at : 8 * (at + 1), :] + far[8 * at : 8 * (at + 1), :]
    coefficients(raw, east, same, other, range(0, HALO, UNIT))
    places = tiles(0, HALO)
    kept = [
        copy_of(source.at[..., places, :], target, sem_out.at[place])
        for place, (source, target) in enumerate(
            ((c, c_far), (e, e_far), (east, east_far), (same, same_far), (other, other_far))
        )
    ]
    for copy in kept:
        copy.start()
    for copy in fetched[:4]:
        copy.wait()

    def complete(section, src):
        for parity in range(2):
            src[parity, tiles(HALO + section, 2), :] = saved[parity, pl.ds(16 * section, 16), :]

    spans = [(step, step + HALO) for step in range(1, STEPS + 1)]
    diffuse(values, spare, east, same, other, spans, joined=False, before_step=complete)
    fetched[4].wait()
    multiply(values, e, product, range(STEPS, STEPS + HALO, UNIT))
    lay_out(product, plain, mine, other_core)
    for copy in kept:
        copy.wait()


def forcing_kernel(parts, weight, innovation, out, *increment, scale):
    total = parts[0]
    for block in range(1, parts.shape[0]):
        total = total + parts[block]
    total = scale * total
    if increment:
        increment[0][...] = total[:2]
    forcing = weight[...] * (total - innovation[...])
    for block in range(out.shape[0]):
        out[block] = forcing


def fetch(sources, targets, sems):
    inside, outside = tiles(HALO, SPAN - HALO), tiles(0, HALO)
    waits = []
    for place, (target, (inner, far)) in enumerate(zip(targets, sources)):
        pair = (
            copy_of(inner.at[..., inside, :], target.at[..., inside, :], sems.at[2 * place]),
            copy_of(far, target.at[..., outside, :], sems.at[2 * place + 1]),
        )
        for copy in pair:
            copy.start()
        waits.append(pair)

    def wait(place):
        for copy in waits[place]:
            copy.wait()

    return wait


def gradient(wait, e, east, same, other, values, spare, scale, lo):
    wait(0)
    for at in blocks_from(lo):
        for parity in range(2):
            term = get(e.at[parity], at, UNIT) * get(values.at[parity], at, UNIT)
            put(values.at[parity], at, scale * term)
    for place in (1, 2, 3):
        wait(place)
    diffuse(values, spare, east, same, other, inward(lo))


def middle_kernel(mine, other_core, e_in, e_far, east_in, east_far, same_in, same_far, other_in, other_far,
                  c_in, c_far, mine_out, other_out, c_hbm,
                  values, spare, plain, e, east, same, other, c, c_new, sems, sem_out, *, scale):
    sources = ((e_in, e_far), (east_in, east_far), (same_in, same_far), (other_in, other_far), (c_in, c_far))
    wait = fetch(sources, (e, east, same, other, c), sems)
    spread(mine, other_core, plain, values)
    gradient(wait, e, east, same, other, values, spare, scale, STEPS)
    wait(4)
    for at in blocks_from(2 * STEPS):
        for parity in range(2):
            new = get(c.at[parity], at, UNIT)
            new = new - step_size * (new + get(values.at[parity], at, UNIT))
            put(c_new.at[parity], at, new)
            put(values.at[parity], at, new)
    inside = tiles(HALO, SPAN - HALO)
    keep = copy_of(c_new.at[:, inside, :], c_hbm, sem_out)
    keep.start()
    diffuse(values, spare, east, same, other, inward(2 * STEPS))
    multiply(values, e, spare, blocks_from(3 * STEPS))
    lay_out(spare, plain, mine_out, other_out)
    keep.wait()


def last_kernel(mine, other_core, e_in, e_far, east_in, east_far, same_in, same_far, other_in, other_far,
                c_in, out_hbm, values, spare, plain, e, east, same, other, c, out, sems, sem_in, sem_out, *, scale):
    inside = tiles(HALO, SPAN - HALO)
    last = copy_of(c_in, c.at[:, inside, :], sem_in)
    sources = ((e_in, e_far), (east_in, east_far), (same_in, same_far), (other_in, other_far))
    wait = fetch(sources, (e, east, same, other), sems)
    last.start()
    spread(mine, other_core, plain, values)
    gradient(wait, e, east, same, other, values, spare, scale, 3 * STEPS)
    last.wait()
    for at in blocks_from(HALO):
        for parity in range(2):
            new = get(c.at[parity], at, UNIT)
            put(values.at[parity], at, new - step_size * (new + get(values.at[parity], at, UNIT)))
    copies = []
    for member in range(2):
        for level in range(2):
            for parity in range(2):
                part = band_of(values.at[parity], 2 * member + level)
                out[member, level, pl.ds(parity, 128, stride=2), :] = part.T
            copy = copy_of(out.at[member, level], out_hbm.at[member, level], sem_out.at[2 * member + level])
            copy.start()
            copies.append(copy)
    for copy in copies:
        copy.wait()


def near_core(value):
    return pltpu.with_memory_space_constraint(value, pltpu.VMEM)


def call(kernel, outs, scratch, name, *args, far_in=(), far_out=()):
    here, far = pl.BlockSpec(memory_space=pltpu.VMEM), pl.BlockSpec(memory_space=pl.ANY)
    copied = not all(isinstance(part, tuple) for part in scratch)
    return pl.pallas_call(
        kernel,
        out_shape=[
            (jax.ShapeDtypeStruct if place in far_out else pltpu.VMEM)(shape, jnp.float32)
            for place, shape in enumerate(outs)
        ],
        in_specs=[far if place in far_in else here for place in range(len(args))],
        out_specs=[far if place in far_out and copied else here for place in range(len(outs))],
        scratch_shapes=[pltpu.VMEM(part, jnp.float32) if isinstance(part, tuple) else part for part in scratch],
        name=name,
    )(*args)


def swap_chips(parts):
    size = lax.axis_size("mem")
    groups = [list(range(core, size, 2)) for core in range(2)]
    return lax.all_to_all(parts, "mem", split_axis=0, concat_axis=0, tiled=True, axis_index_groups=groups)


def swap_cores(part):
    return lax.ppermute(part, "mem", [(i, i ^ 1) for i in range(lax.axis_size("mem"))])


def swap_bands(part, odd_up):
    bands = lax.axis_size("lon")
    return lax.ppermute(part, "lon", [(i, (i + 1 if (i % 2 == 1) == odd_up else i - 1) % bands) for i in range(bands)])


def body(ensemble, controls_start, kappa_east, kappa_north, innovation, obs_mask, gauge_index, gauge_precision):
    chips = lax.axis_size("mem") // 2
    scale = float(lax.axis_size("mem") * ensemble.shape[0]) ** (-0.5)
    field, one, plain = (2, 8 * SIZE, 128), (8 * SIZE, 128), (3, 256, 128)
    far_field, far_one, band = (2, 8 * HALO, 128), (8 * HALO, 128), (2, 8 * (SPAN - HALO), 128)
    parcel, parts, local, wide = (8 * SENT, 128), (chips, 3, 8, 128), (3, 8, 128), (256, 128)
    sem = pltpu.SemaphoreType.DMA
    w, innov, first, second = call(
        edges_kernel, (innovation.shape, innovation.shape, parcel, parcel), (parcel, parcel, wide), "edges",
        controls_start, ensemble, kappa_east, kappa_north, innovation, obs_mask, gauge_index,
        gauge_precision.reshape(1, GAUGES),
    )
    near, far = near_core(swap_bands(first, True)), near_core(swap_bands(second, False))
    c, e, east, same, other, product, saved = call(
        inner_kernel, (field, field, field, one, one, field, (2, 8 * (2 * STEPS + 1), 128)), (field, field, field, wide),
        "inner", controls_start, ensemble, kappa_east, kappa_north, far_out=range(6),
    )
    w, innov, saved = near_core(w), near_core(innov), near_core(saved)
    mine, theirs, weight, innov, c_far, e_far, east_far, same_far, other_far = call(
        outer_kernel, (parts, parts, local, local, far_field, far_field, far_field, far_one, far_one),
        (field, field, plain, field, field, field, field, field, one, one, sem((5,)), sem((5,))), "outer",
        near, far, w, innov, saved, e, east, same, other, product, far_in=range(5, 10), far_out=range(4, 9),
    )
    weight, innov = near_core(weight), near_core(innov)
    fixed = (e, e_far, east, east_far, same, same_far, other, other_far)

    def forced(mine, theirs, outs):
        kernel = lambda *refs: forcing_kernel(*refs, scale=scale)
        sums = near_core(swap_chips(mine + swap_cores(theirs)))
        forcing, *increment = call(kernel, outs, (), "forcing", sums, weight, innov)
        mine = swap_chips(forcing)
        return near_core(mine), near_core(swap_cores(mine)), *increment

    mine, theirs = forced(mine, theirs, (parts,))
    kernel = lambda *refs: middle_kernel(*refs, scale=scale)
    mine, theirs, c = call(
        kernel, (parts, parts, band), (field, field, plain, field, field, one, one, field, field, sem((10,)), sem),
        "middle", mine, theirs, *fixed, c, c_far, far_in=range(2, 12), far_out=(2,),
    )
    mine, theirs, increment = forced(mine, theirs, (parts, innovation.shape))
    kernel = lambda *refs: last_kernel(*refs, scale=scale)
    (controls,) = call(
        kernel, (controls_start.shape,),
        (field, field, plain, field, field, one, one, field, controls_start.shape, sem((8,)), sem, sem((4,))),
        "last", mine, theirs, *fixed, c, far_in=range(2, 11), far_out=(0,),
    )
    return controls, increment


def solution(mesh):
    in_specs = (
        P("mem", None, None, "lon"),
        P("mem", None, None, "lon"),
        P(None, None, "lon"),
        P(None, None, "lon"),
        P(None, "mem", "lon"),
        P(None, "mem", "lon"),
        P(None, "mem", "lon"),
        P(),
    )
    out_specs = (P("mem", None, None, "lon"), P(None, "mem", "lon"))
    return jax.shard_map(body, mesh=mesh, in_specs=in_specs, out_specs=out_specs, check_vma=False)
```

time: 124 us -> 105 us (0.85)
  waiting for transfers between devices: 16.1 us -> 7.93 us
  Pallas kernels: 34.5 us -> 27.1 us
  other arithmetic: 1.9 us -> 0.04 us
  local copies, waits for them, and re-layouts: 2.16 us -> 0.6 us
    pallas_call x6 -> x7, Pallas kernels: 34.5 us -> 27.1 us  [call(): pl.pallas_call(kernel, out_shape=[(jax.ShapeDtypeStruct if place in far_o...]
    ppermute x2, waiting for transfers between devices: 11.4 us -> 4.25 us  [swap_bands(): lax.ppermute(part, 'lon', [(i, (i + 1 if (i % 2 == 1) == odd_up else i -...]
    add x2, other arithmetic: 1.9 us -> 0.04 us  [forced(): sums = near_core(swap_chips(mine + swap_cores(theirs)))]
    unnamed x12 -> x1, local copies, waits for them, and re-layouts: 2.16 us -> 0.6 us
  transfers between devices with their start and end apart: 6 -> 6, of which waited for: 5 -> 5; matrix products, arithmetic and copies ran while one was open for 0% -> 1% of each run, Pallas kernels for 0% -> 7%
where the time goes in v3:
time: 105 us; the launch traced here: 104 us
  blocking collectives  51 us (49%)
  Pallas kernels  27.1 us (26%)
  starting transfers between devices  16.9 us (16%)
  waiting for transfers between devices  7.93 us (8%)
    all_to_all x4, blocking collectives, swap_chips(): lax.all_to_all(parts, 'mem', split_axis=0, concat_axis=0, tiled=True, axi...  51 us
    pallas_call x7, Pallas kernels, call(): pl.pallas_call(kernel, out_shape=[(jax.ShapeDtypeStruct if place in far_o...  27.1 us
    ppermute x2, starting transfers between devices, swap_bands(): lax.ppermute(part, 'lon', [(i, (i + 1 if (i % 2 == 1) == odd_up else i -...  10 us
    ppermute x4, starting transfers between devices, swap_cores(): lax.ppermute(part, 'mem', [(i, i ^ 1) for i in range(lax.axis_size('mem'))])  6.91 us
    ppermute x2, waiting for transfers between devices, swap_bands(): lax.ppermute(part, 'lon', [(i, (i + 1 if (i % 2 == 1) == odd_up else i -...  4.25 us
    ppermute x4, waiting for transfers between devices, swap_cores(): lax.ppermute(part, 'mem', [(i, i ^ 1) for i in range(lax.axis_size('mem'))])  3.68 us
  transfers between devices with their start and end apart: 6, of which 5 were waited for; matrix products, arithmetic and copies ran while one was open for 1% of the time, Pallas kernels for 7%

profile of v3, /device:TPU:1, one launch (start us, length us, event | category | flops | bytes accessed | tf_op | source)
XLA Modules:
  0.0 104.2 jit_solution(4974683276169370377)
XLA Ops:
  0.6 2.0 %edges.1 = (f32[2,8,128]{2,1,0:T(8,128)S(1)}, f32[2,8,128]{2,1,0:T(8,128)S(1)}, f32[544,128]{1,0:T(8,128)S(1)}, f32[544,128]{1,0:T(8,128)S(1)}) custom-call(f32[2,2,256,128]{3,2,1,0:T(8,128)} %controls.3, bf16[2,2,256,128]{3,2,1,0:T(8,128)(2,1)} %ensemble.3, f32[2,256,128]{2,1,0:T(8,128)} %kappa_east.3, f32[2,256,128]{2,1,0:T(8,128)} %kappa_north.3, ...), custom_call_target="tpu_custom_call" | custom-call | tf_op jit(solution)/shard_map/edges/pallas_call | solution.py:419
  2.7 10.0 %collective-permute-start = (f32[544,128]{1,0:T(8,128)S(1)}, f32[544,128]{1,0:T(8,128)S(1)}, u32[]{:S(2)}, u32[]{:S(2)}) collective-permute-start(f32[544,128]{1,0:T(8,128)S(1)} %get-tuple-element.27), channel_id=1, source_target_pairs={{0,7},{1,2},{2,1},{3,4},{4,3},{5,6},{6,5},{7,0},{8,15},{9,10},{10,... | collective-permute-start | bytes 835592 | tf_op jit(solution)/shard_map/ppermute | solution.py:444
  12.7 0.0 collective-permute-start.1
  12.7 6.8 %inner.1 = (f32[2,720,128]{2,1,0:T(8,128)}, f32[2,720,128]{2,1,0:T(8,128)}, f32[2,720,128]{2,1,0:T(8,128)}, f32[720,128]{1,0:T(8,128)}, f32[720,128]{1,0:T(8,128...) custom-call(f32[2,2,256,128]{3,2,1,0:T(8,128)} %controls.3, bf16[2,2,256,128]{3,2,1,0:T(8,128)(2,1)} %ensemble.3, ...), custom_call_target="tpu_custom_call" | custom-call | tf_op jit(solution)/shard_map/inner/pallas_call | solution.py:419
  19.5 4.2 %collective-permute-done.near = f32[544,128]{1,0:T(8,128)S(1)} collective-permute-done((f32[544,128]{1,0:T(8,128)S(1)}, f32[544,128]{1,0:T(8,128)S(1)}, u32[]{:S(2)}, u32[]{:S(2)}) %collective-permute-start) | collective-permute-done | bytes 278560 | tf_op jit(solution)/shard_map/ppermute | solution.py:444
  23.8 0.0 collective-permute-done.1.far
  23.8 2.2 %outer.1 = (f32[16,3,8,128]{3,2,1,0:T(8,128)S(1)}, f32[16,3,8,128]{3,2,1,0:T(8,128)S(1)}, f32[3,8,128]{2,1,0:T(8,128)S(1)}, f32[3,8,128]{2,1,0:T(8,128)S(1)}, f3...) custom-call(f32[544,128]{1,0:T(8,128)S(1)} %collective-permute-done., ...), custom_call_target="tpu_custom_call" | custom-call | tf_op jit(solution)/shard_map/outer/pallas_call | solution.py:419
  26.0 1.7 %collective-permute-start.2 = (f32[16,3,8,128]{3,2,1,0:T(8,128)S(1)}, f32[16,3,8,128]{3,2,1,0:T(8,128)S(1)}, u32[]{:S(2)}, u32[]{:S(2)}) collective-permute-start(f32[16,3,8,128]{3,2,1,0:T(8,128)S(1)} %get-tuple-element.38), channel_id=1, source_target_pairs={{0,8},{8,0},{16,24},{24,16},{32,40},{40,32},{48,56},{56,48},{64,72... | collective-permute-start | bytes 589832 | tf_op jit(solution)/shard_map/ppermute | solution.py:439
  27.7 1.1 %collective-permute-done.2 = f32[16,3,8,128]{3,2,1,0:T(8,128)S(1)} collective-permute-done((f32[16,3,8,128]{3,2,1,0:T(8,128)S(1)}, f32[16,3,8,128]{3,2,1,0:T(8,128)S(1)}, u32[]{:S(2)}, u32[]{:S(2)}) %collective-permute-start.2) | collective-permute-done | bytes 196640 | tf_op jit(solution)/shard_map/ppermute | solution.py:439
  28.8 15.1 %all_to_all.20.refs_0_ = f32[16,3,8,128]{3,2,1,0:T(8,128)S(1)} all-to-all(f32[16,3,8,128]{3,2,1,0:T(8,128)S(1)} %add.6), channel_id=1, replica_groups={{0,16,32,48,64,80,96,112,128,144,160,176,192,208,224,240},{8,24,40,56,7..., dimensions={0} | all-to-all | bytes 393216 | tf_op jit(solution)/shard_map/all_to_all | solution.py:435
  43.9 12.1 %all_to_all.21.refs_0_ = f32[16,3,8,128]{3,2,1,0:T(8,128)S(1)} all-to-all(f32[16,3,8,128]{3,2,1,0:T(8,128)S(1)} %forcing.2), channel_id=1, replica_groups={{0,16,32,48,64,80,96,112,128,144,160,176,192,208,224,240},{8,24,40,56,7..., dimensions={0} | all-to-all | bytes 393216 | tf_op jit(solution)/shard_map/all_to_all | solution.py:435
  56.0 2.4 %collective-permute-start.3 = (f32[16,3,8,128]{3,2,1,0:T(8,128)S(1)}, f32[16,3,8,128]{3,2,1,0:T(8,128)S(1)}, u32[]{:S(2)}, u32[]{:S(2)}) collective-permute-start(f32[16,3,8,128]{3,2,1,0:T(8,128)S(1)} %all_to_all.21.refs_0_), channel_id=1, source_target_pairs={{0,8},{8,0},{16,24},{24,16},{32,40},{40,32},{48,56},{56,48},{64,72... | collective-permute-start | bytes 589832 | tf_op jit(solution)/shard_map/ppermute | solution.py:439
  58.3 1.1 %collective-permute-done.3.refs_1_ = f32[16,3,8,128]{3,2,1,0:T(8,128)S(1)} collective-permute-done((f32[16,3,8,128]{3,2,1,0:T(8,128)S(1)}, f32[16,3,8,128]{3,2,1,0:T(8,128)S(1)}, u32[]{:S(2)}, u32[]{:S(2)}) %collective-permute-start.3) | collective-permute-done | bytes 196640 | tf_op jit(solution)/shard_map/ppermute | solution.py:439
  59.4 10.2 %middle.1 = (f32[16,3,8,128]{3,2,1,0:T(8,128)S(1)}, f32[16,3,8,128]{3,2,1,0:T(8,128)S(1)}, f32[2,512,128]{2,1,0:T(8,128)}) custom-call(f32[16,3,8,128]{3,2,1,0:T(8,128)S(1)} %all_to_all.21.refs_0_, f32[16,3,8,128]{3,2,1,0:T(8,128)S(1)} %collective-permute-done.3.refs_1_, f32[2,720,128]{2,1,0:T(8,128)} %get-tuple-element.32.e_hbm.refs_2_, ...), custom_call_target="tpu_custom_call" | custom-call | tf_op jit(solution)/shard_map/middle/pallas_call | solution.py:419
  69.6 0.5 collective-permute-start.4
  70.1 1.1 %collective-permute-done.4 = f32[16,3,8,128]{3,2,1,0:T(8,128)S(1)} collective-permute-done((f32[16,3,8,128]{3,2,1,0:T(8,128)S(1)}, f32[16,3,8,128]{3,2,1,0:T(8,128)S(1)}, u32[]{:S(2)}, u32[]{:S(2)}) %collective-permute-start.4) | collective-permute-done | bytes 196640 | tf_op jit(solution)/shard_map/ppermute | solution.py:439
  71.2 11.8 %all_to_all.22.refs_0_ = f32[16,3,8,128]{3,2,1,0:T(8,128)S(1)} all-to-all(f32[16,3,8,128]{3,2,1,0:T(8,128)S(1)} %add.7), channel_id=1, replica_groups={{0,16,32,48,64,80,96,112,128,144,160,176,192,208,224,240},{8,24,40,56,7..., dimensions={0} | all-to-all | bytes 393216 | tf_op jit(solution)/shard_map/all_to_all | solution.py:435
  83.0 12.1 %all_to_all.23.refs_0_ = f32[16,3,8,128]{3,2,1,0:T(8,128)S(1)} all-to-all(f32[16,3,8,128]{3,2,1,0:T(8,128)S(1)} %get-tuple-element.49), channel_id=1, replica_groups={{0,16,32,48,64,80,96,112,128,144,160,176,192,208,224,240},{8,24,40,56,7..., dimensions={0} | all-to-all | bytes 393216 | tf_op jit(solution)/shard_map/all_to_all | solution.py:435
  95.0 2.4 %collective-permute-start.5 = (f32[16,3,8,128]{3,2,1,0:T(8,128)S(1)}, f32[16,3,8,128]{3,2,1,0:T(8,128)S(1)}, u32[]{:S(2)}, u32[]{:S(2)}) collective-permute-start(f32[16,3,8,128]{3,2,1,0:T(8,128)S(1)} %all_to_all.23.refs_0_), channel_id=1, source_target_pairs={{0,8},{8,0},{16,24},{24,16},{32,40},{40,32},{48,56},{56,48},{64,72... | collective-permute-start | bytes 589832 | tf_op jit(solution)/shard_map/ppermute | solution.py:439
  97.4 0.6 copy.10
  98.0 0.5 collective-permute-done.5.refs_1_
  98.5 5.8 %last.1 = f32[2,2,256,128]{3,2,1,0:T(8,128)} custom-call(f32[16,3,8,128]{3,2,1,0:T(8,128)S(1)} %all_to_all.23.refs_0_, f32[16,3,8,128]{3,2,1,0:T(8,128)S(1)} %collective-permute-done.5.refs_1_, f32[2,720,128]{2,1,0:T(8,128)} %get-tuple-element.32.e_hbm.refs_2_, f32[2,192,128]{2,1,0:T(8,128)} %get-tuple-element.41.refs_3_, ...), custom_call_target="tpu_custom_call" | custom-call | tf_op jit(solution)/shard_map/last/pallas_call | solution.py:419
  (4 shorter events, 0.1 us)
Async XLA Ops:
  2.7 21.1 %collective-permute-start = (f32[544,128]{1,0:T(8,128)S(1)}, f32[544,128]{1,0:T(8,128)S(1)}, u32[]{:S(2)}, u32[]{:S(2)}) collective-permute-start(f32[544,128]{1,0:T(8,128)S(1)} %get-tuple-element.27), channel_id=1, source_target_pairs={{0,7},{1,2},{2,1},{3,4},{4,3},{5,6},{6,5},{7,0},{8,15},{9,10},{10,... | collective-permute-start | bytes 835592 | tf_op jit(solution)/shard_map/ppermute | solution.py:444
  12.7 11.1 %collective-permute-start.1 = (f32[544,128]{1,0:T(8,128)S(1)}, f32[544,128]{1,0:T(8,128)S(1)}, u32[]{:S(2)}, u32[]{:S(2)}) collective-permute-start(f32[544,128]{1,0:T(8,128)S(1)} %get-tuple-element.28), channel_id=1, source_target_pairs={{0,1},{1,0},{2,3},{3,2},{4,5},{5,4},{6,7},{7,6},{8,9},{9,8},{10,11... | collective-permute-start | bytes 835592 | tf_op jit(solution)/shard_map/ppermute | solution.py:444
  26.0 2.8 %collective-permute-start.2 = (f32[16,3,8,128]{3,2,1,0:T(8,128)S(1)}, f32[16,3,8,128]{3,2,1,0:T(8,128)S(1)}, u32[]{:S(2)}, u32[]{:S(2)}) collective-permute-start(f32[16,3,8,128]{3,2,1,0:T(8,128)S(1)} %get-tuple-element.38), channel_id=1, source_target_pairs={{0,8},{8,0},{16,24},{24,16},{32,40},{40,32},{48,56},{56,48},{64,72... | collective-permute-start | bytes 589832 | tf_op jit(solution)/shard_map/ppermute | solution.py:439
  56.0 3.4 %collective-permute-start.3 = (f32[16,3,8,128]{3,2,1,0:T(8,128)S(1)}, f32[16,3,8,128]{3,2,1,0:T(8,128)S(1)}, u32[]{:S(2)}, u32[]{:S(2)}) collective-permute-start(f32[16,3,8,128]{3,2,1,0:T(8,128)S(1)} %all_to_all.21.refs_0_), channel_id=1, source_target_pairs={{0,8},{8,0},{16,24},{24,16},{32,40},{40,32},{48,56},{56,48},{64,72... | collective-permute-start | bytes 589832 | tf_op jit(solution)/shard_map/ppermute | solution.py:439
  69.6 1.5 %collective-permute-start.4 = (f32[16,3,8,128]{3,2,1,0:T(8,128)S(1)}, f32[16,3,8,128]{3,2,1,0:T(8,128)S(1)}, u32[]{:S(2)}, u32[]{:S(2)}) collective-permute-start(f32[16,3,8,128]{3,2,1,0:T(8,128)S(1)} %get-tuple-element.48), channel_id=1, source_target_pairs={{0,8},{8,0},{16,24},{24,16},{32,40},{40,32},{48,56},{56,48},{64,72... | collective-permute-start | bytes 589832 | tf_op jit(solution)/shard_map/ppermute | solution.py:439
  95.0 3.4 %collective-permute-start.5 = (f32[16,3,8,128]{3,2,1,0:T(8,128)S(1)}, f32[16,3,8,128]{3,2,1,0:T(8,128)S(1)}, u32[]{:S(2)}, u32[]{:S(2)}) collective-permute-start(f32[16,3,8,128]{3,2,1,0:T(8,128)S(1)} %all_to_all.23.refs_0_), channel_id=1, source_target_pairs={{0,8},{8,0},{16,24},{24,16},{32,40},{40,32},{48,56},{56,48},{64,72... | collective-permute-start | bytes 589832 | tf_op jit(solution)/shard_map/ppermute | solution.py:439

commit v4 on v3

--- a/solution.py
+++ b/solution.py
@@ -16,6 +16,7 @@
 SPAN = HALO + BAND // 2
 SIZE = PAD + SPAN + PAD
 UNIT = 8
+LEAD, LAG = 6, 6
 SENT = 2 * HALO + REACH + 2
 
 
@@ -71,40 +72,56 @@
 
 
 def diffuse(source, spare, east, same, other, spans, joined=True, before_step=None):
-    def opening(src, first):
-        before = []
-        for parity in range(2):
-            pair = get(src.at[parity], first - 1, 2)
-            before.append(get(east.at[parity], first - 1, 1) * (pair[1:] - pair[:1]))
-        return pltpu.roll(get(src.at[0], first, UNIT), 127, 2), *before
-
     if joined:
         for parity in range(2):
             join(source.at[parity])
-    carry = opening(source, spans[0][0])
-    for section, (first, end) in enumerate(spans):
-        src, dst = (source, spare) if section % 2 == 0 else (spare, source)
-        if before_step is not None:
-            before_step(section, src)
-        ahead, *before = carry
-        for at in range(first, end, UNIT):
-            even, odd = (get(src.at[parity], at, UNIT + 1) for parity in range(2))
-            across = get(other, at, UNIT) * (ahead - odd[:-1])
-            back = pltpu.roll(across, 1, 2)
-            if at + UNIT < end:
-                ahead = pltpu.roll(get(src.at[0], at + UNIT, UNIT), 127, 2)
-            elif section + 1 < STEPS:
-                carry = opening(dst, spans[section + 1][0])
-            within = get(same, at, UNIT) * (odd[:-1] - even[:-1])
-            for parity, values in ((1, odd), (0, even)):
-                flux = get(east.at[parity], at, UNIT) * (values[1:] - values[:-1])
-                change = flux - jnp.concatenate([before[parity], flux[:-1]], axis=0)
-                north = across - within if parity else within - back
-                put(dst.at[parity], at, (values[:-1] + change) + north)
-                before[parity] = flux[-1:]
-        if joined:
+    stream = [(section, place) for section, (first, end) in enumerate(spans) for place in range(first, end)]
+    ends = (source, spare)
+    ahead, open_places, before, values = {}, {}, [None, None], [None, None]
+
+    def turn(item):
+        section, place = stream[item]
+        ahead[item] = pltpu.roll(get(ends[section % 2].at[0], place, 1), 127, 2)
+
+    def finish(item):
+        section, place = stream[item]
+        dst = ends[(section + 1) % 2]
+        part, back = open_places.pop(item)
+        put(dst.at[0], place, part - back)
+        if joined and place == SPAN - 1:
             for parity in range(2):
                 join(dst.at[parity])
+
+    for item in range(LEAD):
+        turn(item)
+    for item, (section, place) in enumerate(stream):
+        src, dst = ends[section % 2], ends[(section + 1) % 2]
+        if place == spans[section][0]:
+            if before_step is not None:
+                before_step(section, src)
+            for parity in range(2):
+                values[parity] = get(src.at[parity], place, 1)
+                face = values[parity] - get(src.at[parity], place - 1, 1)
+                before[parity] = get(east.at[parity], place - 1, 1) * face
+        if item + LEAD < len(stream):
+            turn(item + LEAD)
+        even, odd = values
+        across = get(other, place, 1) * (ahead.pop(item) - odd)
+        back = pltpu.roll(across, 1, 2)
+        within = get(same, place, 1) * (odd - even)
+        for parity, north in ((0, within), (1, across - within)):
+            after = get(src.at[parity], place + 1, 1)
+            flux = get(east.at[parity], place, 1) * (after - values[parity])
+            new = (values[parity] + (flux - before[parity])) + north
+            before[parity], values[parity] = flux, after
+            if parity:
+                put(dst.at[1], place, new)
+            else:
+                open_places[item] = (new, back)
+        if item >= LAG:
+            finish(item - LAG)
+    for item in range(len(stream) - LAG, len(stream)):
+        finish(item)
 
 
 def inward(lo):
@@ -123,10 +140,10 @@
     for member in range(2):
         for level in range(2):
             row = 2 * member + level
-            wide[...] = ensemble[member, level].astype(jnp.float32)
+            wide[row] = ensemble[member, level].astype(jnp.float32)
             for parity in range(2):
                 send(controls[member, level, pl.ds(parity, 128, stride=2), :], 0, 4 * parity + row)
-                send(wide[pl.ds(parity, 128, stride=2), :], HALO + REACH, 4 * parity + row)
+                send(wide[row, pl.ds(parity, 128, stride=2), :], HALO + REACH, 4 * parity + row)
     for kind, kappa in enumerate((kappa_east, kappa_north)):
         for level in range(2):
             for parity in range(2):
@@ -190,10 +207,10 @@
     for member in range(2):
         for level in range(2):
             row = 2 * member + level
-            wide[...] = ensemble[member, level].astype(jnp.float32)
+            wide[row] = ensemble[member, level].astype(jnp.float32)
             for parity in range(2):
                 lay(controls[member, level, pl.ds(parity, 128, stride=2), :], parity, row, c_out, values)
-                lay(wide[pl.ds(parity, 128, stride=2), :], parity, row, e_out)
+                lay(wide[row, pl.ds(parity, 128, stride=2), :], parity, row, e_out)
     for kind, kappa in enumerate((kappa_east, kappa_north)):
         for level in range(2):
             for parity in range(2):
@@ -233,47 +250,73 @@
         at += 1
 
 
-def block_rows(chip, own):
+def own_rows():
     core = lax.axis_index("mem") % 2
-    if not own:
-        core = 1 - core
-    return pl.ds(pl.multiple_of(16 * chip + 8 * core, 8), 8)
-
-
-def lay_out(product, plain, mine, other_core):
-    for parity in range(2):
-        edges = []
-        for level in range(2):
-            plain[level, pl.ds(parity, 128, stride=2), :] = band_of(product.at[parity], level).T
-            for half in range(2):
-                edges.append(product[parity, rows(0, level + 4 * half, 32), :])
-        plain[2, pl.ds(parity, 128, stride=2), :] = jnp.concatenate(edges, axis=0).T
+    return (row_index()[0] < 4) == (core == 0)
+
+
+def grouped(block):
+    place = lax.broadcasted_iota(jnp.int32, block.shape, block.ndim - 2)
+    block = jnp.take_along_axis(block, (2 * place) % 8 + place // 4, axis=block.ndim - 2)
+    core = lax.axis_index("mem") % 2
+    return jnp.where(core == 0, block, pltpu.roll(block, 4, block.ndim - 2))
+
+
+def ungrouped(block):
+    core = lax.axis_index("mem") % 2
+    block = jnp.where(core == 0, block, pltpu.roll(block, 4, block.ndim - 2))
+    place = lax.broadcasted_iota(jnp.int32, block.shape, block.ndim - 2)
+    return jnp.take_along_axis(block, place // 2 + 4 * (place % 2), axis=block.ndim - 2)
+
+
+def lay_out(product, mine, other_core):
+    own = own_rows()
     for tile in range(3):
+        turned = []
+        for parity in range(2):
+            if tile < 2:
+                part = band_of(product.at[parity], tile)
+            else:
+                part = jnp.concatenate(
+                    [product[parity, rows(0, level + 4 * half, 32), :] for level in range(2) for half in range(2)],
+                    axis=0,
+                )
+            turned.append(part.T)
+        even, odd = turned
         for chip in range(mine.shape[0]):
-            mine[chip, tile] = plain[tile, block_rows(chip, True), :]
-            other_core[chip, tile] = plain[tile, block_rows(chip, False), :]
-
-
-def spread(mine, other_core, plain, forcing):
+            here = slice(8 * chip, 8 * (chip + 1))
+            other = pltpu.roll(odd[here], 4, 0)
+            mine[chip, tile] = jnp.where(own, even[here], other)
+            other_core[chip, tile] = jnp.where(own, other, even[here])
+
+
+def spread(mine, other_core, forcing):
+    own = own_rows()
     for tile in range(3):
+        parts = ([], [])
         for chip in range(mine.shape[0]):
-            plain[tile, block_rows(chip, True), :] = mine[chip, tile]
-            plain[tile, block_rows(chip, False), :] = other_core[chip, tile]
-    for parity in range(2):
-        edges = plain[2, pl.ds(parity, 128, stride=2), :].T
-        for level in range(2):
-            halves = halves_of(plain[level, pl.ds(parity, 128, stride=2), :].T)
-            for half in range(2):
-                edge = edges[64 * level + 32 * half : 64 * level + 32 * half + HALO]
+            one, two = mine[chip, tile], other_core[chip, tile]
+            parts[0].append(jnp.where(own, one, two))
+            parts[1].append(pltpu.roll(jnp.where(own, two, one), 4, 0))
+        for parity in range(2):
+            turned = jnp.concatenate(parts[parity], axis=0).T
+            if tile < 2:
+                pieces = [(tile, half, HALO, part) for half, part in enumerate(halves_of(turned))]
+            else:
+                pieces = [
+                    (level, half, 0, turned[64 * level + 32 * half : 64 * level + 32 * half + HALO])
+                    for level in range(2)
+                    for half in range(2)
+                ]
+            for level, half, place, part in pieces:
                 for member in range(2):
                     row = 4 * half + 2 * member + level
-                    forcing[parity, rows(0, row, HALO), :] = edge
-                    forcing[parity, rows(HALO, row, 64), :] = halves[half]
+                    forcing[parity, rows(place, row, part.shape[0]), :] = part
 
 
 def outer_kernel(near, far, w_in, i_in, saved, e_hbm, east_hbm, same_hbm, other_hbm, product_hbm,
                  mine, other_core, w_out, i_out, c_far, e_far, east_far, same_far, other_far,
-                 values, spare, plain, product, raw, c, e, east, same, other, sem_in, sem_out):
+                 values, spare, product, raw, c, e, east, same, other, sem_in, sem_out):
     edge, rest = tiles(HALO, UNIT), tiles(HALO + STEPS, SPAN - HALO - STEPS)
     fetched = [
         copy_of(source.at[..., edge, :], target.at[..., edge, :], sem_in.at[place])
@@ -312,7 +355,7 @@
     diffuse(values, spare, east, same, other, spans, joined=False, before_step=complete)
     fetched[4].wait()
     multiply(values, e, product, range(STEPS, STEPS + HALO, UNIT))
-    lay_out(product, plain, mine, other_core)
+    lay_out(product, mine, other_core)
     for copy in kept:
         copy.wait()
 
@@ -321,10 +364,10 @@
     total = parts[0]
     for block in range(1, parts.shape[0]):
         total = total + parts[block]
-    total = scale * total
+    total = ungrouped(scale * total)
     if increment:
         increment[0][...] = total[:2]
-    forcing = weight[...] * (total - innovation[...])
+    forcing = grouped(weight[...] * (total - innovation[...]))
     for block in range(out.shape[0]):
         out[block] = forcing
 
@@ -361,10 +404,10 @@
 
 def middle_kernel(mine, other_core, e_in, e_far, east_in, east_far, same_in, same_far, other_in, other_far,
                   c_in, c_far, mine_out, other_out, c_hbm,
-                  values, spare, plain, e, east, same, other, c, c_new, sems, sem_out, *, scale):
+                  values, spare, e, east, same, other, c, c_new, sems, sem_out, *, scale):
     sources = ((e_in, e_far), (east_in, east_far), (same_in, same_far), (other_in, other_far), (c_in, c_far))
     wait = fetch(sources, (e, east, same, other, c), sems)
-    spread(mine, other_core, plain, values)
+    spread(mine, other_core, values)
     gradient(wait, e, east, same, other, values, spare, scale, STEPS)
     wait(4)
     for at in blocks_from(2 * STEPS):
@@ -378,18 +421,18 @@
     keep.start()
     diffuse(values, spare, east, same, other, inward(2 * STEPS))
     multiply(values, e, spare, blocks_from(3 * STEPS))
-    lay_out(spare, plain, mine_out, other_out)
+    lay_out(spare, mine_out, other_out)
     keep.wait()
 
 
 def last_kernel(mine, other_core, e_in, e_far, east_in, east_far, same_in, same_far, other_in, other_far,
-                c_in, out_hbm, values, spare, plain, e, east, same, other, c, out, sems, sem_in, sem_out, *, scale):
+                c_in, out_hbm, values, spare, e, east, same, other, c, out, sems, sem_in, sem_out, *, scale):
     inside = tiles(HALO, SPAN - HALO)
     last = copy_of(c_in, c.at[:, inside, :], sem_in)
     sources = ((e_in, e_far), (east_in, east_far), (same_in, same_far), (other_in, other_far))
     wait = fetch(sources, (e, east, same, other), sems)
     last.start()
-    spread(mine, other_core, plain, values)
+    spread(mine, other_core, values)
     gradient(wait, e, east, same, other, values, spare, scale, 3 * STEPS)
     last.wait()
     for at in blocks_from(HALO):
@@ -447,9 +490,9 @@
 def body(ensemble, controls_start, kappa_east, kappa_north, innovation, obs_mask, gauge_index, gauge_precision):
     chips = lax.axis_size("mem") // 2
     scale = float(lax.axis_size("mem") * ensemble.shape[0]) ** (-0.5)
-    field, one, plain = (2, 8 * SIZE, 128), (8 * SIZE, 128), (3, 256, 128)
+    field, one = (2, 8 * SIZE, 128), (8 * SIZE, 128)
     far_field, far_one, band = (2, 8 * HALO, 128), (8 * HALO, 128), (2, 8 * (SPAN - HALO), 128)
-    parcel, parts, local, wide = (8 * SENT, 128), (chips, 3, 8, 128), (3, 8, 128), (256, 128)
+    parcel, parts, local, wide = (8 * SENT, 128), (chips, 3, 8, 128), (3, 8, 128), (4, 256, 128)
     sem = pltpu.SemaphoreType.DMA
     w, innov, first, second = call(
         edges_kernel, (innovation.shape, innovation.shape, parcel, parcel), (parcel, parcel, wide), "edges",
@@ -464,7 +507,7 @@
     w, innov, saved = near_core(w), near_core(innov), near_core(saved)
     mine, theirs, weight, innov, c_far, e_far, east_far, same_far, other_far = call(
         outer_kernel, (parts, parts, local, local, far_field, far_field, far_field, far_one, far_one),
-        (field, field, plain, field, field, field, field, field, one, one, sem((5,)), sem((5,))), "outer",
+        (field, field, field, field, field, field, field, one, one, sem((5,)), sem((5,))), "outer",
         near, far, w, innov, saved, e, east, same, other, product, far_in=range(5, 10), far_out=range(4, 9),
     )
     weight, innov = near_core(weight), near_core(innov)
@@ -480,14 +523,14 @@
     mine, theirs = forced(mine, theirs, (parts,))
     kernel = lambda *refs: middle_kernel(*refs, scale=scale)
     mine, theirs, c = call(
-        kernel, (parts, parts, band), (field, field, plain, field, field, one, one, field, field, sem((10,)), sem),
+        kernel, (parts, parts, band), (field, field, field, field, one, one, field, field, sem((10,)), sem),
         "middle", mine, theirs, *fixed, c, c_far, far_in=range(2, 12), far_out=(2,),
     )
     mine, theirs, increment = forced(mine, theirs, (parts, innovation.shape))
     kernel = lambda *refs: last_kernel(*refs, scale=scale)
     (controls,) = call(
         kernel, (controls_start.shape,),
-        (field, field, plain, field, field, one, one, field, controls_start.shape, sem((8,)), sem, sem((4,))),
+        (field, field, field, field, one, one, field, controls_start.shape, sem((8,)), sem, sem((4,))),
         "last", mine, theirs, *fixed, c, far_in=range(2, 11), far_out=(0,),
     )
     return controls, increment

time: 105 us -> 96.7 us (0.921)
  Pallas kernels: 27.1 us -> 17.1 us
  waiting for transfers between devices: 7.93 us -> 10.1 us
    pallas_call x7, Pallas kernels: 27.1 us -> 17.1 us  [call(): pl.pallas_call(kernel, out_shape=[(jax.ShapeDtypeStruct if place in far_o...]
    ppermute x2, waiting for transfers between devices: 4.25 us -> 6.37 us  [swap_bands(): lax.ppermute(part, 'lon', [(i, (i + 1 if (i % 2 == 1) == odd_up else i -...]
  transfers between devices with their start and end apart: 6 -> 6, of which waited for: 5 -> 5; matrix products, arithmetic and copies ran while one was open for 1% -> 1% of each run, Pallas kernels for 7% -> 5%
where the time goes in v4:
time: 96.7 us; the launch traced here: 96.4 us
  blocking collectives  51 us (53%)
  Pallas kernels  17.1 us (18%)
  starting transfers between devices  16.9 us (17%)
  waiting for transfers between devices  10.1 us (10%)
    all_to_all x4, blocking collectives, swap_chips(): lax.all_to_all(parts, 'mem', split_axis=0, concat_axis=0, tiled=True, axi...  51 us
    pallas_call x7, Pallas kernels, call(): pl.pallas_call(kernel, out_shape=[(jax.ShapeDtypeStruct if place in far_o...  17.1 us
    ppermute x2, starting transfers between devices, swap_bands(): lax.ppermute(part, 'lon', [(i, (i + 1 if (i % 2 == 1) == odd_up else i -...  10 us
    ppermute x4, starting transfers between devices, swap_cores(): lax.ppermute(part, 'mem', [(i, i ^ 1) for i in range(lax.axis_size('mem'))])  6.91 us
    ppermute x2, waiting for transfers between devices, swap_bands(): lax.ppermute(part, 'lon', [(i, (i + 1 if (i % 2 == 1) == odd_up else i -...  6.37 us
    ppermute x4, waiting for transfers between devices, swap_cores(): lax.ppermute(part, 'mem', [(i, i ^ 1) for i in range(lax.axis_size('mem'))])  3.68 us
  transfers between devices with their start and end apart: 6, of which 5 were waited for; matrix products, arithmetic and copies ran while one was open for 1% of the time, Pallas kernels for 5%

profile of v4, /device:TPU:1, one launch (start us, length us, event | category | flops | bytes accessed | tf_op | source)
XLA Modules:
  0.0 96.4 jit_solution(4385579374764867824)
XLA Ops:
  0.6 2.0 %edges.1 = (f32[2,8,128]{2,1,0:T(8,128)S(1)}, f32[2,8,128]{2,1,0:T(8,128)S(1)}, f32[544,128]{1,0:T(8,128)S(1)}, f32[544,128]{1,0:T(8,128)S(1)}) custom-call(f32[2,2,256,128]{3,2,1,0:T(8,128)} %controls.3, bf16[2,2,256,128]{3,2,1,0:T(8,128)(2,1)} %ensemble.3, f32[2,256,128]{2,1,0:T(8,128)} %kappa_east.3, f32[2,256,128]{2,1,0:T(8,128)} %kappa_north.3, ...), custom_call_target="tpu_custom_call" | custom-call | tf_op jit(solution)/shard_map/edges/pallas_call | solution.py:462
  2.7 10.0 %collective-permute-start = (f32[544,128]{1,0:T(8,128)S(1)}, f32[544,128]{1,0:T(8,128)S(1)}, u32[]{:S(2)}, u32[]{:S(2)}) collective-permute-start(f32[544,128]{1,0:T(8,128)S(1)} %get-tuple-element.27), channel_id=1, source_target_pairs={{0,7},{1,2},{2,1},{3,4},{4,3},{5,6},{6,5},{7,0},{8,15},{9,10},{10,... | collective-permute-start | bytes 835592 | tf_op jit(solution)/shard_map/ppermute | solution.py:487
  12.7 0.0 collective-permute-start.1
  12.7 4.7 %inner.1 = (f32[2,720,128]{2,1,0:T(8,128)}, f32[2,720,128]{2,1,0:T(8,128)}, f32[2,720,128]{2,1,0:T(8,128)}, f32[720,128]{1,0:T(8,128)}, f32[720,128]{1,0:T(8,128...) custom-call(f32[2,2,256,128]{3,2,1,0:T(8,128)} %controls.3, bf16[2,2,256,128]{3,2,1,0:T(8,128)(2,1)} %ensemble.3, ...), custom_call_target="tpu_custom_call" | custom-call | tf_op jit(solution)/shard_map/inner/pallas_call | solution.py:462
  17.4 6.4 %collective-permute-done.near = f32[544,128]{1,0:T(8,128)S(1)} collective-permute-done((f32[544,128]{1,0:T(8,128)S(1)}, f32[544,128]{1,0:T(8,128)S(1)}, u32[]{:S(2)}, u32[]{:S(2)}) %collective-permute-start) | collective-permute-done | bytes 278560 | tf_op jit(solution)/shard_map/ppermute | solution.py:487
  23.8 0.0 collective-permute-done.1.far
  23.8 2.1 %outer.1 = (f32[16,3,8,128]{3,2,1,0:T(8,128)S(1)}, f32[16,3,8,128]{3,2,1,0:T(8,128)S(1)}, f32[3,8,128]{2,1,0:T(8,128)S(1)}, f32[3,8,128]{2,1,0:T(8,128)S(1)}, f3...) custom-call(f32[544,128]{1,0:T(8,128)S(1)} %collective-permute-done., ...), custom_call_target="tpu_custom_call" | custom-call | tf_op jit(solution)/shard_map/outer/pallas_call | solution.py:462
  25.9 1.7 %collective-permute-start.2 = (f32[16,3,8,128]{3,2,1,0:T(8,128)S(1)}, f32[16,3,8,128]{3,2,1,0:T(8,128)S(1)}, u32[]{:S(2)}, u32[]{:S(2)}) collective-permute-start(f32[16,3,8,128]{3,2,1,0:T(8,128)S(1)} %get-tuple-element.38), channel_id=1, source_target_pairs={{0,8},{8,0},{16,24},{24,16},{32,40},{40,32},{48,56},{56,48},{64,72... | collective-permute-start | bytes 589832 | tf_op jit(solution)/shard_map/ppermute | solution.py:482
  27.7 1.1 %collective-permute-done.2 = f32[16,3,8,128]{3,2,1,0:T(8,128)S(1)} collective-permute-done((f32[16,3,8,128]{3,2,1,0:T(8,128)S(1)}, f32[16,3,8,128]{3,2,1,0:T(8,128)S(1)}, u32[]{:S(2)}, u32[]{:S(2)}) %collective-permute-start.2) | collective-permute-done | bytes 196640 | tf_op jit(solution)/shard_map/ppermute | solution.py:482
  28.8 15.1 %all_to_all.20.refs_0_ = f32[16,3,8,128]{3,2,1,0:T(8,128)S(1)} all-to-all(f32[16,3,8,128]{3,2,1,0:T(8,128)S(1)} %add.6), channel_id=1, replica_groups={{0,16,32,48,64,80,96,112,128,144,160,176,192,208,224,240},{8,24,40,56,7..., dimensions={0} | all-to-all | bytes 393216 | tf_op jit(solution)/shard_map/all_to_all | solution.py:478
  43.9 12.1 %all_to_all.21.refs_0_ = f32[16,3,8,128]{3,2,1,0:T(8,128)S(1)} all-to-all(f32[16,3,8,128]{3,2,1,0:T(8,128)S(1)} %forcing.2), channel_id=1, replica_groups={{0,16,32,48,64,80,96,112,128,144,160,176,192,208,224,240},{8,24,40,56,7..., dimensions={0} | all-to-all | bytes 393216 | tf_op jit(solution)/shard_map/all_to_all | solution.py:478
  55.9 2.4 %collective-permute-start.3 = (f32[16,3,8,128]{3,2,1,0:T(8,128)S(1)}, f32[16,3,8,128]{3,2,1,0:T(8,128)S(1)}, u32[]{:S(2)}, u32[]{:S(2)}) collective-permute-start(f32[16,3,8,128]{3,2,1,0:T(8,128)S(1)} %all_to_all.21.refs_0_), channel_id=1, source_target_pairs={{0,8},{8,0},{16,24},{24,16},{32,40},{40,32},{48,56},{56,48},{64,72... | collective-permute-start | bytes 589832 | tf_op jit(solution)/shard_map/ppermute | solution.py:482
  58.3 1.1 %collective-permute-done.3.refs_1_ = f32[16,3,8,128]{3,2,1,0:T(8,128)S(1)} collective-permute-done((f32[16,3,8,128]{3,2,1,0:T(8,128)S(1)}, f32[16,3,8,128]{3,2,1,0:T(8,128)S(1)}, u32[]{:S(2)}, u32[]{:S(2)}) %collective-permute-start.3) | collective-permute-done | bytes 196640 | tf_op jit(solution)/shard_map/ppermute | solution.py:482
  59.4 4.3 %middle.1 = (f32[16,3,8,128]{3,2,1,0:T(8,128)S(1)}, f32[16,3,8,128]{3,2,1,0:T(8,128)S(1)}, f32[2,512,128]{2,1,0:T(8,128)}) custom-call(f32[16,3,8,128]{3,2,1,0:T(8,128)S(1)} %all_to_all.21.refs_0_, f32[16,3,8,128]{3,2,1,0:T(8,128)S(1)} %collective-permute-done.3.refs_1_, f32[2,720,128]{2,1,0:T(8,128)} %get-tuple-element.32.e_hbm.refs_2_, ...), custom_call_target="tpu_custom_call" | custom-call | tf_op jit(solution)/shard_map/middle/pallas_call | solution.py:462
  63.7 0.5 collective-permute-start.4
  64.2 1.1 %collective-permute-done.4 = f32[16,3,8,128]{3,2,1,0:T(8,128)S(1)} collective-permute-done((f32[16,3,8,128]{3,2,1,0:T(8,128)S(1)}, f32[16,3,8,128]{3,2,1,0:T(8,128)S(1)}, u32[]{:S(2)}, u32[]{:S(2)}) %collective-permute-start.4) | collective-permute-done | bytes 196640 | tf_op jit(solution)/shard_map/ppermute | solution.py:482
  65.3 11.8 %all_to_all.22.refs_0_ = f32[16,3,8,128]{3,2,1,0:T(8,128)S(1)} all-to-all(f32[16,3,8,128]{3,2,1,0:T(8,128)S(1)} %add.7), channel_id=1, replica_groups={{0,16,32,48,64,80,96,112,128,144,160,176,192,208,224,240},{8,24,40,56,7..., dimensions={0} | all-to-all | bytes 393216 | tf_op jit(solution)/shard_map/all_to_all | solution.py:478
  77.1 12.1 %all_to_all.23.refs_0_ = f32[16,3,8,128]{3,2,1,0:T(8,128)S(1)} all-to-all(f32[16,3,8,128]{3,2,1,0:T(8,128)S(1)} %get-tuple-element.49), channel_id=1, replica_groups={{0,16,32,48,64,80,96,112,128,144,160,176,192,208,224,240},{8,24,40,56,7..., dimensions={0} | all-to-all | bytes 393216 | tf_op jit(solution)/shard_map/all_to_all | solution.py:478
  89.2 2.4 %collective-permute-start.5 = (f32[16,3,8,128]{3,2,1,0:T(8,128)S(1)}, f32[16,3,8,128]{3,2,1,0:T(8,128)S(1)}, u32[]{:S(2)}, u32[]{:S(2)}) collective-permute-start(f32[16,3,8,128]{3,2,1,0:T(8,128)S(1)} %all_to_all.23.refs_0_), channel_id=1, source_target_pairs={{0,8},{8,0},{16,24},{24,16},{32,40},{40,32},{48,56},{56,48},{64,72... | collective-permute-start | bytes 589832 | tf_op jit(solution)/shard_map/ppermute | solution.py:482
  91.5 0.6 copy.10
  92.1 0.5 collective-permute-done.5.refs_1_
  92.6 3.8 %last.1 = f32[2,2,256,128]{3,2,1,0:T(8,128)} custom-call(f32[16,3,8,128]{3,2,1,0:T(8,128)S(1)} %all_to_all.23.refs_0_, f32[16,3,8,128]{3,2,1,0:T(8,128)S(1)} %collective-permute-done.5.refs_1_, f32[2,720,128]{2,1,0:T(8,128)} %get-tuple-element.32.e_hbm.refs_2_, f32[2,192,128]{2,1,0:T(8,128)} %get-tuple-element.41.refs_3_, ...), custom_call_target="tpu_custom_call" | custom-call | tf_op jit(solution)/shard_map/last/pallas_call | solution.py:462
  (4 shorter events, 0.1 us)
Async XLA Ops:
  2.7 21.1 %collective-permute-start = (f32[544,128]{1,0:T(8,128)S(1)}, f32[544,128]{1,0:T(8,128)S(1)}, u32[]{:S(2)}, u32[]{:S(2)}) collective-permute-start(f32[544,128]{1,0:T(8,128)S(1)} %get-tuple-element.27), channel_id=1, source_target_pairs={{0,7},{1,2},{2,1},{3,4},{4,3},{5,6},{6,5},{7,0},{8,15},{9,10},{10,... | collective-permute-start | bytes 835592 | tf_op jit(solution)/shard_map/ppermute | solution.py:487
  12.7 11.1 %collective-permute-start.1 = (f32[544,128]{1,0:T(8,128)S(1)}, f32[544,128]{1,0:T(8,128)S(1)}, u32[]{:S(2)}, u32[]{:S(2)}) collective-permute-start(f32[544,128]{1,0:T(8,128)S(1)} %get-tuple-element.28), channel_id=1, source_target_pairs={{0,1},{1,0},{2,3},{3,2},{4,5},{5,4},{6,7},{7,6},{8,9},{9,8},{10,11... | collective-permute-start | bytes 835592 | tf_op jit(solution)/shard_map/ppermute | solution.py:487
  25.9 2.8 %collective-permute-start.2 = (f32[16,3,8,128]{3,2,1,0:T(8,128)S(1)}, f32[16,3,8,128]{3,2,1,0:T(8,128)S(1)}, u32[]{:S(2)}, u32[]{:S(2)}) collective-permute-start(f32[16,3,8,128]{3,2,1,0:T(8,128)S(1)} %get-tuple-element.38), channel_id=1, source_target_pairs={{0,8},{8,0},{16,24},{24,16},{32,40},{40,32},{48,56},{56,48},{64,72... | collective-permute-start | bytes 589832 | tf_op jit(solution)/shard_map/ppermute | solution.py:482
  55.9 3.4 %collective-permute-start.3 = (f32[16,3,8,128]{3,2,1,0:T(8,128)S(1)}, f32[16,3,8,128]{3,2,1,0:T(8,128)S(1)}, u32[]{:S(2)}, u32[]{:S(2)}) collective-permute-start(f32[16,3,8,128]{3,2,1,0:T(8,128)S(1)} %all_to_all.21.refs_0_), channel_id=1, source_target_pairs={{0,8},{8,0},{16,24},{24,16},{32,40},{40,32},{48,56},{56,48},{64,72... | collective-permute-start | bytes 589832 | tf_op jit(solution)/shard_map/ppermute | solution.py:482
  63.7 1.5 %collective-permute-start.4 = (f32[16,3,8,128]{3,2,1,0:T(8,128)S(1)}, f32[16,3,8,128]{3,2,1,0:T(8,128)S(1)}, u32[]{:S(2)}, u32[]{:S(2)}) collective-permute-start(f32[16,3,8,128]{3,2,1,0:T(8,128)S(1)} %get-tuple-element.48), channel_id=1, source_target_pairs={{0,8},{8,0},{16,24},{24,16},{32,40},{40,32},{48,56},{56,48},{64,72... | collective-permute-start | bytes 589832 | tf_op jit(solution)/shard_map/ppermute | solution.py:482
  89.2 3.4 %collective-permute-start.5 = (f32[16,3,8,128]{3,2,1,0:T(8,128)S(1)}, f32[16,3,8,128]{3,2,1,0:T(8,128)S(1)}, u32[]{:S(2)}, u32[]{:S(2)}) collective-permute-start(f32[16,3,8,128]{3,2,1,0:T(8,128)S(1)} %all_to_all.23.refs_0_), channel_id=1, source_target_pairs={{0,8},{8,0},{16,24},{24,16},{32,40},{40,32},{48,56},{56,48},{64,72... | collective-permute-start | bytes 589832 | tf_op jit(solution)/shard_map/ppermute | solution.py:482

commit v5 on v4

--- a/solution.py
+++ b/solution.py
@@ -125,7 +125,7 @@
 
 
 def inward(lo):
-    return [(blocks_from(lo + step)[0], SPAN) for step in range(1, STEPS + 1)]
+    return [(lo + step, SPAN) for step in range(1, STEPS + 1)]
 
 
 def edges_kernel(controls, ensemble, kappa_east, kappa_north, innovation, mask, gauge, precision,

time: 96.7 us -> 97.5 us (level)
  no operation moved by 1% of the time
where the time goes in v5:
time: 97.5 us; the launch traced here: 97.1 us
  blocking collectives  51 us (52%)
  Pallas kernels  17.8 us (18%)
  starting transfers between devices  16.9 us (17%)
  waiting for transfers between devices  10.1 us (10%)
    all_to_all x4, blocking collectives, swap_chips(): lax.all_to_all(parts, 'mem', split_axis=0, concat_axis=0, tiled=True, axi...  51 us
    pallas_call x7, Pallas kernels, call(): pl.pallas_call(kernel, out_shape=[(jax.ShapeDtypeStruct if place in far_o...  17.8 us
    ppermute x2, starting transfers between devices, swap_bands(): lax.ppermute(part, 'lon', [(i, (i + 1 if (i % 2 == 1) == odd_up else i -...  10 us
    ppermute x4, starting transfers between devices, swap_cores(): lax.ppermute(part, 'mem', [(i, i ^ 1) for i in range(lax.axis_size('mem'))])  6.91 us
    ppermute x2, waiting for transfers between devices, swap_bands(): lax.ppermute(part, 'lon', [(i, (i + 1 if (i % 2 == 1) == odd_up else i -...  6.37 us
    ppermute x4, waiting for transfers between devices, swap_cores(): lax.ppermute(part, 'mem', [(i, i ^ 1) for i in range(lax.axis_size('mem'))])  3.68 us
  transfers between devices with their start and end apart: 6, of which 5 were waited for; matrix products, arithmetic and copies ran while one was open for 1% of the time, Pallas kernels for 5%

profile of v5, /device:TPU:1, one launch (start us, length us, event | category | flops | bytes accessed | tf_op | source)
XLA Modules:
  0.0 97.1 jit_solution(16038963455417793491)
XLA Ops:
  0.6 2.0 %edges.1 = (f32[2,8,128]{2,1,0:T(8,128)S(1)}, f32[2,8,128]{2,1,0:T(8,128)S(1)}, f32[544,128]{1,0:T(8,128)S(1)}, f32[544,128]{1,0:T(8,128)S(1)}) custom-call(f32[2,2,256,128]{3,2,1,0:T(8,128)} %controls.3, bf16[2,2,256,128]{3,2,1,0:T(8,128)(2,1)} %ensemble.3, f32[2,256,128]{2,1,0:T(8,128)} %kappa_east.3, f32[2,256,128]{2,1,0:T(8,128)} %kappa_north.3, ...), custom_call_target="tpu_custom_call" | custom-call | tf_op jit(solution)/shard_map/edges/pallas_call | solution.py:462
  2.7 10.0 %collective-permute-start = (f32[544,128]{1,0:T(8,128)S(1)}, f32[544,128]{1,0:T(8,128)S(1)}, u32[]{:S(2)}, u32[]{:S(2)}) collective-permute-start(f32[544,128]{1,0:T(8,128)S(1)} %get-tuple-element.27), channel_id=1, source_target_pairs={{0,7},{1,2},{2,1},{3,4},{4,3},{5,6},{6,5},{7,0},{8,15},{9,10},{10,... | collective-permute-start | bytes 835592 | tf_op jit(solution)/shard_map/ppermute | solution.py:487
  12.7 0.0 collective-permute-start.1
  12.7 4.7 %inner.1 = (f32[2,720,128]{2,1,0:T(8,128)}, f32[2,720,128]{2,1,0:T(8,128)}, f32[2,720,128]{2,1,0:T(8,128)}, f32[720,128]{1,0:T(8,128)}, f32[720,128]{1,0:T(8,128...) custom-call(f32[2,2,256,128]{3,2,1,0:T(8,128)} %controls.3, bf16[2,2,256,128]{3,2,1,0:T(8,128)(2,1)} %ensemble.3, ...), custom_call_target="tpu_custom_call" | custom-call | tf_op jit(solution)/shard_map/inner/pallas_call | solution.py:462
  17.4 6.4 %collective-permute-done.near = f32[544,128]{1,0:T(8,128)S(1)} collective-permute-done((f32[544,128]{1,0:T(8,128)S(1)}, f32[544,128]{1,0:T(8,128)S(1)}, u32[]{:S(2)}, u32[]{:S(2)}) %collective-permute-start) | collective-permute-done | bytes 278560 | tf_op jit(solution)/shard_map/ppermute | solution.py:487
  23.8 0.0 collective-permute-done.1.far
  23.8 2.1 %outer.1 = (f32[16,3,8,128]{3,2,1,0:T(8,128)S(1)}, f32[16,3,8,128]{3,2,1,0:T(8,128)S(1)}, f32[3,8,128]{2,1,0:T(8,128)S(1)}, f32[3,8,128]{2,1,0:T(8,128)S(1)}, f3...) custom-call(f32[544,128]{1,0:T(8,128)S(1)} %collective-permute-done., ...), custom_call_target="tpu_custom_call" | custom-call | tf_op jit(solution)/shard_map/outer/pallas_call | solution.py:462
  25.9 1.7 %collective-permute-start.2 = (f32[16,3,8,128]{3,2,1,0:T(8,128)S(1)}, f32[16,3,8,128]{3,2,1,0:T(8,128)S(1)}, u32[]{:S(2)}, u32[]{:S(2)}) collective-permute-start(f32[16,3,8,128]{3,2,1,0:T(8,128)S(1)} %get-tuple-element.38), channel_id=1, source_target_pairs={{0,8},{8,0},{16,24},{24,16},{32,40},{40,32},{48,56},{56,48},{64,72... | collective-permute-start | bytes 589832 | tf_op jit(solution)/shard_map/ppermute | solution.py:482
  27.7 1.1 %collective-permute-done.2 = f32[16,3,8,128]{3,2,1,0:T(8,128)S(1)} collective-permute-done((f32[16,3,8,128]{3,2,1,0:T(8,128)S(1)}, f32[16,3,8,128]{3,2,1,0:T(8,128)S(1)}, u32[]{:S(2)}, u32[]{:S(2)}) %collective-permute-start.2) | collective-permute-done | bytes 196640 | tf_op jit(solution)/shard_map/ppermute | solution.py:482
  28.8 15.1 %all_to_all.20.refs_0_ = f32[16,3,8,128]{3,2,1,0:T(8,128)S(1)} all-to-all(f32[16,3,8,128]{3,2,1,0:T(8,128)S(1)} %add.6), channel_id=1, replica_groups={{0,16,32,48,64,80,96,112,128,144,160,176,192,208,224,240},{8,24,40,56,7..., dimensions={0} | all-to-all | bytes 393216 | tf_op jit(solution)/shard_map/all_to_all | solution.py:478
  43.9 12.1 %all_to_all.21.refs_0_ = f32[16,3,8,128]{3,2,1,0:T(8,128)S(1)} all-to-all(f32[16,3,8,128]{3,2,1,0:T(8,128)S(1)} %forcing.2), channel_id=1, replica_groups={{0,16,32,48,64,80,96,112,128,144,160,176,192,208,224,240},{8,24,40,56,7..., dimensions={0} | all-to-all | bytes 393216 | tf_op jit(solution)/shard_map/all_to_all | solution.py:478
  55.9 2.4 %collective-permute-start.3 = (f32[16,3,8,128]{3,2,1,0:T(8,128)S(1)}, f32[16,3,8,128]{3,2,1,0:T(8,128)S(1)}, u32[]{:S(2)}, u32[]{:S(2)}) collective-permute-start(f32[16,3,8,128]{3,2,1,0:T(8,128)S(1)} %all_to_all.21.refs_0_), channel_id=1, source_target_pairs={{0,8},{8,0},{16,24},{24,16},{32,40},{40,32},{48,56},{56,48},{64,72... | collective-permute-start | bytes 589832 | tf_op jit(solution)/shard_map/ppermute | solution.py:482
  58.3 1.1 %collective-permute-done.3.refs_1_ = f32[16,3,8,128]{3,2,1,0:T(8,128)S(1)} collective-permute-done((f32[16,3,8,128]{3,2,1,0:T(8,128)S(1)}, f32[16,3,8,128]{3,2,1,0:T(8,128)S(1)}, u32[]{:S(2)}, u32[]{:S(2)}) %collective-permute-start.3) | collective-permute-done | bytes 196640 | tf_op jit(solution)/shard_map/ppermute | solution.py:482
  59.4 5.0 %middle.1 = (f32[16,3,8,128]{3,2,1,0:T(8,128)S(1)}, f32[16,3,8,128]{3,2,1,0:T(8,128)S(1)}, f32[2,512,128]{2,1,0:T(8,128)}) custom-call(f32[16,3,8,128]{3,2,1,0:T(8,128)S(1)} %all_to_all.21.refs_0_, f32[16,3,8,128]{3,2,1,0:T(8,128)S(1)} %collective-permute-done.3.refs_1_, f32[2,720,128]{2,1,0:T(8,128)} %get-tuple-element.32.e_hbm.refs_2_, ...), custom_call_target="tpu_custom_call" | custom-call | tf_op jit(solution)/shard_map/middle/pallas_call | solution.py:462
  64.4 0.5 collective-permute-start.4
  64.9 1.1 %collective-permute-done.4 = f32[16,3,8,128]{3,2,1,0:T(8,128)S(1)} collective-permute-done((f32[16,3,8,128]{3,2,1,0:T(8,128)S(1)}, f32[16,3,8,128]{3,2,1,0:T(8,128)S(1)}, u32[]{:S(2)}, u32[]{:S(2)}) %collective-permute-start.4) | collective-permute-done | bytes 196640 | tf_op jit(solution)/shard_map/ppermute | solution.py:482
  66.0 11.8 %all_to_all.22.refs_0_ = f32[16,3,8,128]{3,2,1,0:T(8,128)S(1)} all-to-all(f32[16,3,8,128]{3,2,1,0:T(8,128)S(1)} %add.7), channel_id=1, replica_groups={{0,16,32,48,64,80,96,112,128,144,160,176,192,208,224,240},{8,24,40,56,7..., dimensions={0} | all-to-all | bytes 393216 | tf_op jit(solution)/shard_map/all_to_all | solution.py:478
  77.8 12.1 %all_to_all.23.refs_0_ = f32[16,3,8,128]{3,2,1,0:T(8,128)S(1)} all-to-all(f32[16,3,8,128]{3,2,1,0:T(8,128)S(1)} %get-tuple-element.49), channel_id=1, replica_groups={{0,16,32,48,64,80,96,112,128,144,160,176,192,208,224,240},{8,24,40,56,7..., dimensions={0} | all-to-all | bytes 393216 | tf_op jit(solution)/shard_map/all_to_all | solution.py:478
  89.9 2.4 %collective-permute-start.5 = (f32[16,3,8,128]{3,2,1,0:T(8,128)S(1)}, f32[16,3,8,128]{3,2,1,0:T(8,128)S(1)}, u32[]{:S(2)}, u32[]{:S(2)}) collective-permute-start(f32[16,3,8,128]{3,2,1,0:T(8,128)S(1)} %all_to_all.23.refs_0_), channel_id=1, source_target_pairs={{0,8},{8,0},{16,24},{24,16},{32,40},{40,32},{48,56},{56,48},{64,72... | collective-permute-start | bytes 589832 | tf_op jit(solution)/shard_map/ppermute | solution.py:482
  92.2 0.6 copy.10
  92.8 0.5 collective-permute-done.5.refs_1_
  93.3 3.8 %last.1 = f32[2,2,256,128]{3,2,1,0:T(8,128)} custom-call(f32[16,3,8,128]{3,2,1,0:T(8,128)S(1)} %all_to_all.23.refs_0_, f32[16,3,8,128]{3,2,1,0:T(8,128)S(1)} %collective-permute-done.5.refs_1_, f32[2,720,128]{2,1,0:T(8,128)} %get-tuple-element.32.e_hbm.refs_2_, f32[2,192,128]{2,1,0:T(8,128)} %get-tuple-element.41.refs_3_, ...), custom_call_target="tpu_custom_call" | custom-call | tf_op jit(solution)/shard_map/last/pallas_call | solution.py:462
  (4 shorter events, 0.1 us)
Async XLA Ops:
  2.7 21.1 %collective-permute-start = (f32[544,128]{1,0:T(8,128)S(1)}, f32[544,128]{1,0:T(8,128)S(1)}, u32[]{:S(2)}, u32[]{:S(2)}) collective-permute-start(f32[544,128]{1,0:T(8,128)S(1)} %get-tuple-element.27), channel_id=1, source_target_pairs={{0,7},{1,2},{2,1},{3,4},{4,3},{5,6},{6,5},{7,0},{8,15},{9,10},{10,... | collective-permute-start | bytes 835592 | tf_op jit(solution)/shard_map/ppermute | solution.py:487
  12.7 11.1 %collective-permute-start.1 = (f32[544,128]{1,0:T(8,128)S(1)}, f32[544,128]{1,0:T(8,128)S(1)}, u32[]{:S(2)}, u32[]{:S(2)}) collective-permute-start(f32[544,128]{1,0:T(8,128)S(1)} %get-tuple-element.28), channel_id=1, source_target_pairs={{0,1},{1,0},{2,3},{3,2},{4,5},{5,4},{6,7},{7,6},{8,9},{9,8},{10,11... | collective-permute-start | bytes 835592 | tf_op jit(solution)/shard_map/ppermute | solution.py:487
  25.9 2.8 %collective-permute-start.2 = (f32[16,3,8,128]{3,2,1,0:T(8,128)S(1)}, f32[16,3,8,128]{3,2,1,0:T(8,128)S(1)}, u32[]{:S(2)}, u32[]{:S(2)}) collective-permute-start(f32[16,3,8,128]{3,2,1,0:T(8,128)S(1)} %get-tuple-element.38), channel_id=1, source_target_pairs={{0,8},{8,0},{16,24},{24,16},{32,40},{40,32},{48,56},{56,48},{64,72... | collective-permute-start | bytes 589832 | tf_op jit(solution)/shard_map/ppermute | solution.py:482
  55.9 3.4 %collective-permute-start.3 = (f32[16,3,8,128]{3,2,1,0:T(8,128)S(1)}, f32[16,3,8,128]{3,2,1,0:T(8,128)S(1)}, u32[]{:S(2)}, u32[]{:S(2)}) collective-permute-start(f32[16,3,8,128]{3,2,1,0:T(8,128)S(1)} %all_to_all.21.refs_0_), channel_id=1, source_target_pairs={{0,8},{8,0},{16,24},{24,16},{32,40},{40,32},{48,56},{56,48},{64,72... | collective-permute-start | bytes 589832 | tf_op jit(solution)/shard_map/ppermute | solution.py:482
  64.4 1.5 %collective-permute-start.4 = (f32[16,3,8,128]{3,2,1,0:T(8,128)S(1)}, f32[16,3,8,128]{3,2,1,0:T(8,128)S(1)}, u32[]{:S(2)}, u32[]{:S(2)}) collective-permute-start(f32[16,3,8,128]{3,2,1,0:T(8,128)S(1)} %get-tuple-element.48), channel_id=1, source_target_pairs={{0,8},{8,0},{16,24},{24,16},{32,40},{40,32},{48,56},{56,48},{64,72... | collective-permute-start | bytes 589832 | tf_op jit(solution)/shard_map/ppermute | solution.py:482
  89.9 3.4 %collective-permute-start.5 = (f32[16,3,8,128]{3,2,1,0:T(8,128)S(1)}, f32[16,3,8,128]{3,2,1,0:T(8,128)S(1)}, u32[]{:S(2)}, u32[]{:S(2)}) collective-permute-start(f32[16,3,8,128]{3,2,1,0:T(8,128)S(1)} %all_to_all.23.refs_0_), channel_id=1, source_target_pairs={{0,8},{8,0},{16,24},{24,16},{32,40},{40,32},{48,56},{56,48},{64,72... | collective-permute-start | bytes 589832 | tf_op jit(solution)/shard_map/ppermute | solution.py:482
